TPU v7x, 256 devices: a whole 4x4x8 slice. The times are simulated.
256 devices in a mesh: sec: 4 (over z_hi, core), gx: 16 (over z_lo, y), gy: 4 (over x).
Axes of the slice: x: 4, y: 4, z: 8 (z_hi: 2, z_lo: 4; z = z_hi * 4 + z_lo), core: 2. Of those that a mesh axis runs over, the one named last changes fastest.
Arguments:
- fields: float32 [4, 3, 256, 8192], P('sec', None, 'gx', 'gy'), may hold values from -6 to 6
- x_ops: float32 [4, 3, 256, 256], P(None, None, 'gx'), may hold values from -4 to 4, as said below
- y_ops: float32 [4, 3, 256, 256], P(None, None, 'gy'), may hold values from -4 to 4, as said below
- x_line_class: int32 [256], P('gy'), may hold values from 0 to 3
- y_line_class: int32 [256], P('gx'), may hold values from 0 to 3
- box_offset: int32 [3, 2], replicated, may hold values from 0 to 63, as said below
- coupling: float32 [3, 3, 3], replicated, may hold values from -3 to 3
Outputs:
- fields_next: float32 [4, 3, 256, 8192], P('sec', None, 'gx', 'gy')
Inputs may be any that keep to these rules, and one draw needn't show every extreme that they name: `box_offset`: column 0 is below 16 and column 1 below 64; each column reaches its largest value for some box. `x_ops`: A dense matrix for each class and characteristic. `y_ops`: A dense matrix for each class and characteristic.
All inputs are finite; a program needn't handle non-finite values.
Results may differ from a plain program's by a relative error of at most 0.00013.
Values sent between devices are 32-bit elements; how exact they have to be, the bound alone decides.
A program may use at most 64 MiB of HBM per device.

v0:
```python
import jax
import jax.numpy as jnp
from jax import lax
from jax.sharding import PartitionSpec as P

CZ = 32
NCLASS = 4
STEPS = 2


time_step = 0.2
viscosity = 0.25
highest = lax.Precision.HIGHEST


def padded_2(block, sides, width):
    for axis, dim in sides:
        count = lax.axis_size(axis)
        forward = [(i, i + 1) for i in range(count - 1)]
        backward = [(target, source) for source, target in forward]
        low = lax.ppermute(
            lax.slice_in_dim(block, block.shape[dim] - width, None, axis=dim), axis, forward
        )
        high = lax.ppermute(lax.slice_in_dim(block, 0, width, axis=dim), axis, backward)
        block = jnp.concatenate([low, block, high], axis=dim)
    return block


def shifted(value, axis, steps):
    count = lax.axis_size(axis)
    initial, last = (max(0, -steps), min(count, count - steps))
    return lax.ppermute(value, axis, [(source, source + steps) for source in range(initial, last)])


def flow_core(padded):
    centre = padded[:, 1:-1, 1:-1, :]
    ahead_x = padded[:, 2:, 1:-1, :]
    behind_x = padded[:, :-2, 1:-1, :]
    ahead_y = padded[:, 1:-1, 2:, :]
    behind_y = padded[:, 1:-1, :-2, :]
    ahead_z = jnp.roll(centre, -1, axis=3)
    behind_z = jnp.roll(centre, 1, axis=3)
    slope_x = 0.5 * (ahead_x - behind_x)
    slope_y = 0.5 * (ahead_y - behind_y)
    slope_z = 0.5 * (ahead_z - behind_z)
    laplace = ahead_x + behind_x + ahead_y + behind_y + ahead_z + behind_z - 6.0 * centre
    omega_x = slope_y[2] - slope_z[1]
    omega_y = slope_z[0] - slope_x[2]
    omega_z = slope_x[1] - slope_y[0]
    lamb_vector = jnp.stack(
        [
            omega_y * centre[2] - omega_z * centre[1],
            omega_z * centre[0] - omega_x * centre[2],
            omega_x * centre[1] - omega_y * centre[0],
        ]
    )
    updated = centre + time_step * (viscosity * laplace - lamb_vector)
    return (updated, lamb_vector)


def skip_flow(padded):
    centre = padded[:, 1:-1, 1:-1, :]
    return (centre, jnp.zeros_like(centre))


def unchanged(accrued):
    return accrued


def place_source(padded_lamb, offset_x, offset_y, matrix, span_x, span_y, extent_x, extent_y):
    anchor = jnp.zeros((), jnp.int32)
    corner_x = span_x - offset_x - 1
    corner_y = span_y - offset_y - 1
    window = lax.dynamic_slice(
        padded_lamb,
        (anchor, corner_x, corner_y, anchor),
        (3, extent_x + 1, extent_y + 1, padded_lamb.shape[3]),
    )
    averaged = 0.25 * (
        window[:, :-1, :-1] + window[:, 1:, :-1] + window[:, :-1, 1:] + window[:, 1:, 1:]
    )
    return jnp.einsum("kj,jxyz->kxyz", matrix, averaged, precision=highest)


def sweep_lines_x(state, x_ops, select_x, active):
    initial = jnp.zeros(state.shape[1:], jnp.float32)

    def add_piece(running, portion, anchor):

        def work(accrued):
            partial_value = jnp.einsum("ckij,kjl->ckil", x_ops, portion[0], precision=highest)
            return jnp.sum(partial_value * select_x[:, None, None, :], axis=0)

        return lax.cond(active, work, unchanged, running)

    return add_piece(initial, lax.all_gather(state, "gx", axis=2, tiled=True), jnp.int32(0))


def sweep_lines_y(state, y_ops, select_y, active):
    initial = jnp.zeros(state.shape[1:], jnp.float32)

    def add_piece(running, portion, anchor):

        def work(accrued):
            partial_value = jnp.einsum("ckij,kxjz->ckxiz", y_ops, portion[0], precision=highest)
            return jnp.sum(partial_value * select_y[:, None, :, None, None], axis=0)

        return lax.cond(active, work, unchanged, running)

    return add_piece(initial, lax.all_gather(state, "gy", axis=3, tiled=True), jnp.int32(0))


def local(fields, x_ops, y_ops, x_line_class, y_line_class, box_offset, coupling):
    sections = lax.axis_size("sec")
    section_index = lax.axis_index("sec")
    active = section_index == sections - 1
    member = jnp.minimum(section_index, sections - 2)
    span_x = fields.shape[2]
    merged = fields.shape[3]
    span_y = merged // CZ
    classes = jnp.arange(NCLASS, dtype=jnp.int32)
    select_y = (classes[:, None] == y_line_class[None, :]).astype(jnp.float32)
    offsets = lax.dynamic_index_in_dim(box_offset, member, 0, keepdims=False)
    matrix = lax.dynamic_index_in_dim(coupling, member, 0, keepdims=False)
    current = fields[0].reshape(3, span_x, span_y, CZ)
    for repeat in range(STEPS):
        padded = padded_2(current, (("gx", 1), ("gy", 2)), 1)
        flowed, lamb_vector = lax.cond(active, skip_flow, flow_core, padded)
        left_tile = shifted(lamb_vector, "gx", 1)
        joined = jnp.concatenate([left_tile, lamb_vector], axis=1)
        lower_tile = shifted(joined, "gy", 1)
        joined = jnp.concatenate([lower_tile, joined], axis=2)
        contribution = place_source(
            joined, offsets[0], offsets[1], matrix, span_x, span_y, span_x, span_y
        )
        source = lax.psum(contribution, "sec")
        amplitudes_grid = current + time_step * source
        planes = amplitudes_grid.shape[3]
        merged_now = span_y * planes
        select_x = jnp.broadcast_to(
            (classes[:, None, None] == x_line_class[None, :, None]).astype(jnp.float32),
            (NCLASS, span_y, planes),
        ).reshape(NCLASS, merged_now)
        amplitudes = amplitudes_grid.reshape(1, 3, span_x, merged_now)
        swept_x = sweep_lines_x(amplitudes, x_ops, select_x, active)
        swept = sweep_lines_y(
            swept_x.reshape(1, 3, span_x, span_y, planes), y_ops, select_y, active
        )
        current = jnp.where(active, swept, flowed)
    return current.reshape(1, 3, span_x, merged)


def solution(mesh):
    placed = (
        P("sec", None, "gx", "gy"),
        P(None, None, "gx", None),
        P(None, None, "gy", None),
        P("gy"),
        P("gx"),
        P(),
        P(),
    )
    return jax.shard_map(
        local, mesh=mesh, in_specs=placed, out_specs=P("sec", None, "gx", "gy"), check_vma=False
    )
```

profile of v0, /device:TPU:161, one launch (start us, length us, event | category | flops | bytes accessed | tf_op | source)
XLA Modules:
  0.0 695.8 jit_solution(3194117666119599615)
XLA Ops:
  6.5 1.5 reshape_squeeze.6
  8.1 3.2 collective-permute-start
  11.3 4.2 collective-permute-start.1
  15.7 1.4 collective-permute-done.1
  17.2 1.3 collective-permute-start.3
  18.5 4.0 collective-permute-start.2
  22.5 1.4 copy.79
  23.9 1.4 copy.80
  25.3 1.3 copy.78
  26.6 3.1 pad_maximum_fusion.6
  29.7 2.4 conditional.6
  29.7 1.4 copy.124
  31.2 1.0 broadcast.53.clone
  32.2 2.9 collective-permute-start.4
  35.1 12.7 %collective-permute-done.4 = f32[3,16,64,32]{2,3,1,0:T(8,128)S(1)} collective-permute-done((f32[3,16,64,32]{2,3,1,0:T(8,128)}, f32[3,16,64,32]{2,3,1,0:T(8,128)S(1)}, u32[]{:S(2)}, u32[]{:S(2)}) %collective-permute-start.4) | collective-permute-done | bytes 393248 | tf_op jit(solution)/shard_map/ppermute | solution.py:32
  47.9 4.3 collective-permute-start.5
  52.2 0.5 fusion.60
  55.3 13.0 %collective-permute-done.5 = f32[3,32,64,32]{2,3,1,0:T(8,128)} collective-permute-done((f32[3,32,64,32]{2,3,1,0:T(8,128)S(1)}, f32[3,32,64,32]{2,3,1,0:T(8,128)}, u32[]{:S(2)}, u32[]{:S(2)}) %collective-permute-start.5) | collective-permute-done | bytes 786464 | tf_op jit(solution)/shard_map/ppermute | solution.py:32
  68.3 1.7 fusion.41
  70.0 0.5 fusion.43
  70.5 2.2 fusion.38
  72.7 1.0 copy.85
  73.9 0.5 copy.86
  74.4 94.2 %all-reduce.3.cloned.1.call-done = f32[3,16,64,32]{2,3,1,0:T(8,128)} async-done(((f32[3,16,64,32]{2,3,1,0:T(8,128)}), f32[3,16,64,32]{2,3,1,0:T(8,128)}) %all-reduce.3.cloned.1.call-update) | async-done | bytes 393232 | tf_op jit(solution)/shard_map/psum | solution.py:136
  168.6 1.3 multiply_add_fusion.3
  169.9 0.5 copy.87
  170.4 1.5 reshape.56
  172.0 78.3 %all-gather.5.cloned.1.call-done = f32[1,3,256,2048]{3,2,1,0:T(8,128)} async-done(((f32[1,3,16,2048]{3,2,1,0:T(8,128)}), f32[1,3,256,2048]{3,2,1,0:T(8,128)}) %all-gather.5.cloned.1.call-update) | async-done | bytes 6291472 | tf_op jit(solution)/shard_map/all_gather | solution.py:96
  250.4 7.1 %conditional.7 = (f32[3,16,2048]{2,1,0:T(8,128)S(1)}) conditional(s32[]{:T(128)} %convert_element_type.20, () %tuple.48, (f32[1,3,256,2048]{3,2,1,0:T(8,128)}, f32[4,3,16,256]{3,2,1,0:T(8,128)S(1)}, f32[4,64,32]{2,1,0:T(8,128)S(1)}) %tuple.131), branch_computations={%region_3.4_spmd, %region_4.6_spmd} | conditional | flops 1208647680 | bytes 6979592 | solution.py:94
  250.5 6.9 fusion.8
  257.5 1.7 reshape.57
  259.4 73.2 %all-gather.7.cloned.1.call-done = f32[1,3,16,256,32]{4,3,2,1,0:T(8,128)} async-done(((f32[1,3,16,64,32]{4,3,2,1,0:T(8,128)}), f32[1,3,16,256,32]{4,3,2,1,0:T(8,128)}) %all-gather.7.cloned.1.call-update) | async-done | bytes 1572880 | tf_op jit(solution)/shard_map/all_gather | solution.py:110
  332.6 21.9 %conditional.8 = (f32[3,16,64,32]{2,3,1,0:T(8,128)S(1)}) conditional(s32[]{:T(128)} %convert_element_type.20, () %tuple.47, (f32[1,3,16,256,32]{4,3,2,1,0:T(8,128)}, f32[4,3,64,256]{3,2,1,0:T(8,128)S(1)}, f32[4,16]{0,1:T(8,128)S(1)}) %tuple.129), branch_computations={%region_6.7_spmd, %region_7.9_spmd} | conditional | flops 1208647680 | bytes 2752776 | solution.py:108
  332.6 21.9 %fusion.14 = f32[3,16,64,32]{2,3,1,0:T(8,128)S(1)} fusion(f32[1,3,16,256,32]{4,3,2,1,0:T(8,128)} %get-tuple-element.138, f32[4,16]{0,1:T(8,128)S(1)} %get-tuple-element.63, f32[4,3,64,256]{3,2,1,0:T(8,128)S(1)} %get-tuple-element.139), kind=kOutput, calls=%fused_computation.22 | convolution fusion | flops 1208647680 | bytes 2752768 | tf_op jit(solution)/shard_map/cond/branch_1_fun/ckij,kxjz->ckxiz/dot_general | solution.py:105
  354.8 3.1 collective-permute-start.6
  357.9 4.3 collective-permute-start.7
  362.2 1.1 collective-permute-done.7
  363.4 0.9 copy-done.5
  365.0 2.8 collective-permute-start.8
  368.2 1.3 collective-permute-start.9
  369.9 2.9 collective-permute-done.9
  373.2 1.5 pad_maximum_fusion.8
  374.7 0.5 conditional.9
  375.2 2.5 collective-permute-start.10
  377.7 20.7 %collective-permute-done.10 = f32[3,16,64,32]{2,3,1,0:T(8,128)S(1)} collective-permute-done((f32[3,16,64,32]{2,3,1,0:T(8,128)S(1)}, f32[3,16,64,32]{2,3,1,0:T(8,128)S(1)}, u32[]{:S(2)}, u32[]{:S(2)}) %collective-permute-start.10) | collective-permute-done | bytes 393248 | tf_op jit(solution)/shard_map/ppermute | solution.py:32
  398.6 2.9 collective-permute-start.11
  401.5 33.3 %collective-permute-done.11 = f32[3,32,64,32]{2,3,1,0:T(8,128)S(1)} collective-permute-done((f32[3,32,64,32]{2,3,1,0:T(8,128)S(1)}, f32[3,32,64,32]{2,3,1,0:T(8,128)S(1)}, u32[]{:S(2)}, u32[]{:S(2)}) %collective-permute-start.11) | collective-permute-done | bytes 786464 | tf_op jit(solution)/shard_map/ppermute | solution.py:32
  434.8 0.5 fusion.40
  435.3 0.5 fusion.42
  435.8 2.2 fusion.36
  438.0 1.0 copy.103
  439.0 61.7 %all-reduce.5.cloned.1.call-done = f32[3,16,64,32]{2,3,1,0:T(8,128)} async-done(((f32[3,16,64,32]{2,3,1,0:T(8,128)}), f32[3,16,64,32]{2,3,1,0:T(8,128)}) %all-reduce.5.cloned.1.call-update) | async-done | bytes 393232 | tf_op jit(solution)/shard_map/psum | solution.py:136
  500.7 1.3 multiply_add_fusion.2
  502.0 0.5 copy.104
  502.5 1.5 reshape.58
  504.1 78.3 %all-gather.9.cloned.1.call-done = f32[1,3,256,2048]{3,2,1,0:T(8,128)} async-done(((f32[1,3,16,2048]{3,2,1,0:T(8,128)}), f32[1,3,256,2048]{3,2,1,0:T(8,128)}) %all-gather.9.cloned.1.call-update) | async-done | bytes 6291472 | tf_op jit(solution)/shard_map/all_gather | solution.py:96
  582.4 7.2 %conditional.10 = (f32[3,16,2048]{2,1,0:T(8,128)S(1)}) conditional(s32[]{:T(128)} %convert_element_type.20, () %tuple.46, (f32[1,3,256,2048]{3,2,1,0:T(8,128)}, f32[4,3,16,256]{3,2,1,0:T(8,128)S(1)}, f32[4,64,32]{2,1,0:T(8,128)S(1)}) %tuple.132), branch_computations={%region_12.13_spmd, %region_13.15_spmd} | conditional | flops 1208647680 | bytes 6979592 | solution.py:94
  582.7 6.9 fusion.26
  589.6 1.7 reshape.59
  591.4 73.4 %all-gather.11.cloned.1.call-done = f32[1,3,16,256,32]{4,3,2,1,0:T(8,128)} async-done(((f32[1,3,16,64,32]{4,3,2,1,0:T(8,128)}), f32[1,3,16,256,32]{4,3,2,1,0:T(8,128)}) %all-gather.11.cloned.1.call-update) | async-done | bytes 1572880 | tf_op jit(solution)/shard_map/all_gather | solution.py:110
  664.8 21.9 %conditional.11 = (f32[3,16,64,32]{2,3,1,0:T(8,128)S(1)}) conditional(s32[]{:T(128)} %convert_element_type.20, () %tuple.45, (f32[1,3,16,256,32]{4,3,2,1,0:T(8,128)}, f32[4,3,64,256]{3,2,1,0:T(8,128)S(1)}, f32[4,16]{0,1:T(8,128)S(1)}) %tuple.130), branch_computations={%region_15.16_spmd, %region_16.18_spmd} | conditional | flops 1208647680 | bytes 2752776 | solution.py:108
  664.8 21.9 %fusion.32 = f32[3,16,64,32]{2,3,1,0:T(8,128)S(1)} fusion(f32[1,3,16,256,32]{4,3,2,1,0:T(8,128)} %get-tuple-element.147, f32[4,16]{0,1:T(8,128)S(1)} %get-tuple-element.72, f32[4,3,64,256]{3,2,1,0:T(8,128)S(1)} %get-tuple-element.148), kind=kOutput, calls=%fused_computation.46 | convolution fusion | flops 1208647680 | bytes 2752768 | tf_op jit(solution)/shard_map/cond/branch_1_fun/ckij,kxjz->ckxiz/dot_general | solution.py:105
  686.8 0.5 copy.109
  687.3 1.5 reshape.60
  (68 shorter events, 3.9 us)
Async XLA Ops:
  6.5 63.9 %copy-start = (f32[3,3,3]{2,1,0:T(4,128)S(1)}, f32[3,3,3]{2,1,0:T(4,128)}, u32[]{:S(2)}) copy-start(f32[3,3,3]{2,1,0:T(4,128)} %param.25) | copy-start | bytes 328
  6.5 162.0 %all-reduce.3.cloned.1.call-start = ((), (), s32[]{:S(2)}) async-start(), calls=%async_computation | async-start | bytes 1572864 | tf_op jit(solution)/shard_map/psum | solution.py:136
  8.1 7.5 %collective-permute-start = (f32[3,1,64,32]{3,2,1,0:T(8,128)S(1)}, f32[3,1,64,32]{3,2,1,0:T(8,128)S(1)}, u32[]{:S(2)}, u32[]{:S(2)}) collective-permute-start(f32[3,1,64,32]{3,2,1,0:T(8,128)S(1)} %get-tuple-element.180), channel_id=1, source_target_pairs={{0,4},{4,8},{8,12},{12,16},{16,20},{20,24},{24,28},{28,32},{32,36}... | collective-permute-start | bytes 73736 | tf_op jit(solution)/shard_map/ppermute | solution.py:21
  11.3 5.8 collective-permute-start.1
  17.2 6.7 collective-permute-start.3
  18.5 6.8 collective-permute-start.2
  32.2 15.6 %copy-start.11 = (f32[3,16,64,32]{2,3,1,0:T(8,128)S(1)}, f32[3,16,64,32]{2,3,1,0:T(8,128)}, u32[]{:S(2)}) copy-start(f32[3,16,64,32]{2,3,1,0:T(8,128)} %get-tuple-element.150) | copy-start | bytes 1179652
  32.2 20.0 %copy-start.14 = (s32[3,2]{0,1:T(2,128)S(1)}, s32[3,2]{0,1:T(2,128)}, u32[]{:S(2)}) copy-start(s32[3,2]{0,1:T(2,128)} %param.24) | copy-start | bytes 76
  32.2 15.6 %collective-permute-start.4 = (f32[3,16,64,32]{2,3,1,0:T(8,128)}, f32[3,16,64,32]{2,3,1,0:T(8,128)S(1)}, u32[]{:S(2)}, u32[]{:S(2)}) collective-permute-start(f32[3,16,64,32]{2,3,1,0:T(8,128)} %get-tuple-element.150), channel_id=1, source_target_pairs={{0,4},{4,8},{8,12},{12,16},{16,20},{20,24},{24,28},{28,32},{32,36}... | collective-permute-start | bytes 1179656 | tf_op jit(solution)/shard_map/ppermute | solution.py:32
  47.9 20.5 %collective-permute-start.5 = (f32[3,32,64,32]{2,3,1,0:T(8,128)S(1)}, f32[3,32,64,32]{2,3,1,0:T(8,128)}, u32[]{:S(2)}, u32[]{:S(2)}) collective-permute-start(f32[3,32,64,32]{2,3,1,0:T(8,128)S(1)} %constant_dynamic-update-slice_fusion.3), channel_id=1, source_target_pairs={{0,1},{1,2},{2,3},{4,5},{5,6},{6,7},{8,9},{9,10},{10,11},{12,13},{... | collective-permute-start | bytes 2359304 | tf_op jit(solution)/shard_map/ppermute | solution.py:32
  73.7 176.6 %all-gather.5.cloned.1.call-start = ((), (), s32[]{:S(2)}) async-start(), calls=%async_computation.1 | async-start | bytes 6684672 | tf_op jit(solution)/shard_map/all_gather | solution.py:96
  170.4 1.6 copy-start.15
  170.4 80.0 %copy-start.12 = (f32[4,3,16,256]{3,2,1,0:T(8,128)S(1)}, f32[4,3,16,256]{3,2,1,0:T(8,128)}, u32[]{:S(2)}) copy-start(f32[4,3,16,256]{3,2,1,0:T(8,128)} %param.20) | copy-start | bytes 589828
  171.9 160.7 %all-gather.7.cloned.1.call-start = ((), (), s32[]{:S(2)}) async-start(), calls=%async_computation.2 | async-start | bytes 7864320 | tf_op jit(solution)/shard_map/all_gather | solution.py:110
  257.5 1.8 copy-start.16
  257.5 75.1 %copy-start.8 = (f32[4,3,64,256]{3,2,1,0:T(8,128)S(1)}, f32[4,3,64,256]{3,2,1,0:T(8,128)}, u32[]{:S(2)}) copy-start(f32[4,3,64,256]{3,2,1,0:T(8,128)} %param.21) | copy-start | bytes 2359300
  259.3 241.4 %all-reduce.5.cloned.1.call-start = ((), (), s32[]{:S(2)}) async-start(), calls=%async_computation.3 | async-start | bytes 1572864 | tf_op jit(solution)/shard_map/psum | solution.py:136
  332.6 22.0 %copy-start.10 = (f32[3,16,64,32]{2,3,1,0:T(8,128)S(1)}, f32[3,16,64,32]{2,3,1,0:T(8,128)}, u32[]{:S(2)}) copy-start(f32[3,16,64,32]{2,3,1,0:T(8,128)} %get-tuple-element.151) | copy-start | bytes 1179652
  354.7 19.9 %copy-start.3 = (f32[3,16,64,32]{2,3,1,0:T(8,128)}, f32[3,16,64,32]{2,3,1,0:T(8,128)S(1)}, u32[]{:S(2)}) copy-start(f32[3,16,64,32]{2,3,1,0:T(8,128)S(1)} %broadcast_select_fusion.1) | copy-start | bytes 1179652
  354.8 7.4 %collective-permute-start.6 = (f32[3,1,64,32]{2,3,1,0:T(8,128)S(1)}, f32[3,1,64,32]{2,3,1,0:T(8,128)S(1)}, u32[]{:S(2)}, u32[]{:S(2)}) collective-permute-start(f32[3,1,64,32]{2,3,1,0:T(8,128)S(1)} %get-tuple-element.183), channel_id=1, source_target_pairs={{0,4},{4,8},{8,12},{12,16},{16,20},{20,24},{24,28},{28,32},{32,36}... | collective-permute-start | bytes 73736 | tf_op jit(solution)/shard_map/ppermute | solution.py:21
  357.9 5.4 collective-permute-start.7
  363.4 0.9 copy-start.5
  365.0 4.5 collective-permute-start.8
  368.2 4.6 collective-permute-start.9
  375.2 23.3 %collective-permute-start.10 = (f32[3,16,64,32]{2,3,1,0:T(8,128)S(1)}, f32[3,16,64,32]{2,3,1,0:T(8,128)S(1)}, u32[]{:S(2)}, u32[]{:S(2)}) collective-permute-start(f32[3,16,64,32]{2,3,1,0:T(8,128)S(1)} %get-tuple-element.152), channel_id=1, source_target_pairs={{0,4},{4,8},{8,12},{12,16},{16,20},{20,24},{24,28},{28,32},{32,36}... | collective-permute-start | bytes 1179656 | tf_op jit(solution)/shard_map/ppermute | solution.py:32
  398.6 36.2 %collective-permute-start.11 = (f32[3,32,64,32]{2,3,1,0:T(8,128)S(1)}, f32[3,32,64,32]{2,3,1,0:T(8,128)S(1)}, u32[]{:S(2)}, u32[]{:S(2)}) collective-permute-start(f32[3,32,64,32]{2,3,1,0:T(8,128)S(1)} %constant_dynamic-update-slice_fusion.5), channel_id=1, source_target_pairs={{0,1},{1,2},{2,3},{4,5},{5,6},{6,7},{8,9},{9,10},{10,11},{12,13},{... | collective-permute-start | bytes 2359304 | tf_op jit(solution)/shard_map/ppermute | solution.py:32
  437.9 62.7 %copy-start.4 = (f32[3,16,64,32]{2,3,1,0:T(8,128)S(1)}, f32[3,16,64,32]{2,3,1,0:T(8,128)}, u32[]{:S(2)}) copy-start(f32[3,16,64,32]{2,3,1,0:T(8,128)} %copy-done.3) | copy-start | bytes 1179652
  439.0 143.4 %all-gather.9.cloned.1.call-start = ((), (), s32[]{:S(2)}) async-start(), calls=%async_computation.4 | async-start | bytes 6684672 | tf_op jit(solution)/shard_map/all_gather | solution.py:96
  502.5 79.9 %copy-start.13 = (f32[4,3,16,256]{3,2,1,0:T(8,128)S(1)}, f32[4,3,16,256]{3,2,1,0:T(8,128)}, u32[]{:S(2)}) copy-start(f32[4,3,16,256]{3,2,1,0:T(8,128)} %param.20) | copy-start | bytes 589828
  504.0 160.8 %all-gather.11.cloned.1.call-start = ((), (), s32[]{:S(2)}) async-start(), calls=%async_computation.5 | async-start | bytes 7864320 | tf_op jit(solution)/shard_map/all_gather | solution.py:110
  589.6 75.2 %copy-start.9 = (f32[4,3,64,256]{3,2,1,0:T(8,128)S(1)}, f32[4,3,64,256]{3,2,1,0:T(8,128)}, u32[]{:S(2)}) copy-start(f32[4,3,64,256]{3,2,1,0:T(8,128)} %param.21) | copy-start | bytes 2359300
Sparse Core Ops, SparseCore 0:
  73.8 94.7 all-reduce.2
  172.0 78.2 all-gather.4
  259.4 73.1 all-gather.6
  439.1 61.5 all-reduce.4
  504.1 78.2 all-gather.8
  591.5 73.2 all-gather.10
where the time goes:
time: 705 us; the launch traced here: 696 us
  waiting for transfers between devices  544 us (77%)
  matrix products  62.1 us (9%)
  starting transfers between devices  37.1 us (5%)
  local copies, waits for them, and re-layouts  24.3 us (3%)
  between operations  16.6 us (2%)
  other arithmetic  10.8 us (2%)
    all_gather x2, waiting for transfers between devices, sweep_lines_x(): lax.all_gather(state, 'gx', axis=2, tiled=True)  157 us
    psum x2, waiting for transfers between devices, local(): source = lax.psum(contribution, 'sec')  156 us
    all_gather x2, waiting for transfers between devices, sweep_lines_y(): lax.all_gather(state, 'gy', axis=3, tiled=True)  147 us
    ppermute x4, waiting for transfers between devices, shifted(): lax.ppermute(value, axis, [(source, source + steps) for source in range(i...  79.7 us
    dot_general x2, matrix products, work(): jnp.einsum('ckij,kxjz->ckxiz', y_ops, portion[0], precision=highest)  43.8 us
  transfers between devices with their start and end apart: 18, of which 14 were waited for; matrix products, arithmetic and copies ran while one was open for 1% of the time, Pallas kernels for 0%

commit v1 on v0

v1 whole, which is shorter than its diff:
```python
import functools

import jax
import jax.numpy as jnp
from jax import lax
from jax.experimental import pallas as pl
from jax.experimental.pallas import tpu as pltpu
from jax.sharding import PartitionSpec as P

CZ = 32
NCLASS = 4
time_step = 0.2
viscosity = 0.25
MESH = pl.DeviceIdType.MESH
F32 = jnp.float32
BF16 = jnp.bfloat16

DIRS = [(dx, dy) for dx in (-1, 0, 1) for dy in (-1, 0, 1) if (dx, dy) != (0, 0)]


def owner_of(k, q):
    z = (3 * k + 1 + 4 * (q % 2)) % 8
    return 2 * (z // 4) + 1, (z % 4) * 4 + q % 4, q // 4


def roll(value, shift, axis):
    size = value.shape[axis]
    shift = shift % size
    return value if shift == 0 else pltpu.roll(value, shift, axis)


def lanes_of(value):
    return lax.broadcasted_iota(jnp.int32, value.shape, value.ndim - 1)


def swap_blocks(blocks):
    lane = lanes_of(blocks[0])
    blocks = list(blocks)
    for bit in (3, 2, 1, 0):
        d, width = 1 << bit, 2 << bit
        upper = (lane & width) != 0
        for i in range(16):
            if i & d:
                continue
            a, b = blocks[i], blocks[i | d]
            blocks[i] = jnp.where(upper, roll(b, width, 1), a)
            blocks[i | d] = jnp.where(upper, b, roll(a, -width, 1))
    return blocks


def take_lanes(value, index):
    return jnp.take_along_axis(value, index, axis=1, mode="promise_in_bounds")


def to_planes(blocks):
    lane = lanes_of(blocks[0])
    rest = lane % 64
    index = (rest % 4) * 32 + (rest // 4) * 2 + lane // 64
    return [take_lanes(b, index) for b in swap_blocks(blocks)]


def from_planes(blocks):
    lane = lanes_of(blocks[0])
    index = (lane % 2) * 64 + ((lane % 32) // 2) * 4 + lane // 32
    return swap_blocks([take_lanes(b, index) for b in blocks])


def pair_swap(a, b):
    upper = lanes_of(a) >= 64
    return jnp.where(upper, roll(b, 64, 1), a), jnp.where(upper, b, roll(a, 64, 1))


def split(value):
    high = value.astype(BF16)
    return high, (value - high.astype(F32)).astype(BF16)


def dot(a, b):
    return lax.dot_general(a, b, (((1,), (0,)), ((), ())), preferred_element_type=F32)


def flow_block(ref, j, lane):
    def block(c, at):
        return ref[c, :, pl.ds(pl.multiple_of(at * 128, 128), 128)]

    z = lane % CZ
    centre, ax, bx, ay, by, az, bz = [], [], [], [], [], [], []
    for c in range(3):
        cur, prv, nxt = block(c, j), block(c, j - 1), block(c, j + 1)
        centre.append(cur)
        ax.append(roll(cur, -1, 0))
        bx.append(roll(cur, 1, 0))
        ay.append(jnp.where(lane < 96, roll(cur, -32, 1), roll(nxt, -32, 1)))
        by.append(jnp.where(lane >= 32, roll(cur, 32, 1), roll(prv, 32, 1)))
        az.append(jnp.where(z != CZ - 1, roll(cur, -1, 1), roll(cur, 31, 1)))
        bz.append(jnp.where(z != 0, roll(cur, 1, 1), roll(cur, -31, 1)))
    omega_x = 0.5 * ((ay[2] - by[2]) - (az[1] - bz[1]))
    omega_y = 0.5 * ((az[0] - bz[0]) - (ax[2] - bx[2]))
    omega_z = 0.5 * ((ax[1] - bx[1]) - (ay[0] - by[0]))
    u, v, w = centre
    lamb = [omega_y * w - omega_z * v, omega_z * u - omega_x * w, omega_x * v - omega_y * u]
    updated = []
    for c in range(3):
        laplace = ax[c] + bx[c] + ay[c] + by[c] + az[c] + bz[c] - 6.0 * centre[c]
        updated.append(centre[c] + time_step * (viscosity * laplace - lamb[c]))
    return updated, lamb


def kernel(
    coup, off, f, xo, yo, cyl, cxl, out,
    U, V, M, hxs, hxr, hyr, cs, cr, PB, A, L, X, Y, CY, CX, R, Q,
    XH, XL, YH, YL, SX, SY, TH, TL, AH, AL, BH, BL,
    hss, hrs, pss, ars, lrs, xss, yss, css, dss, xrs, yrs, crs, drs, rss, rrs,
):
    sec, gx, gy = lax.axis_index("sec"), lax.axis_index("gx"), lax.axis_index("gy")
    is_flow = sec < 3
    my_q = gy * 4 + gx % 4
    my_z = (sec // 2) * 4 + gx // 4
    my_t = (my_z + 15 - 4 * (my_q % 2)) % 8
    is_owner = (sec % 2 == 1) & (my_t % 3 == 0)
    my_k = my_t // 3

    def remote(src, dst, ss, rs, device):
        return pltpu.make_async_remote_copy(
            src_ref=src, dst_ref=dst, send_sem=ss, recv_sem=rs, device_id=device, device_id_type=MESH
        )

    def inside(dx, dy):
        return (gx + dx >= 0) & (gx + dx < 16) & (gy + dy >= 0) & (gy + dy < 4)

    def halo_copy(n):
        dx, dy = DIRS[n]
        back = DIRS.index((-dx, -dy))
        device = (sec, gx + dx, gy + dy)
        if dy == 0:
            side = 0 if dx > 0 else 1
            return remote(hxs.at[side], hxr.at[side], hss.at[n], hrs.at[back], device)
        if dx == 0:
            side = 0 if dy > 0 else 1
            lanes = pl.ds(1920, 128) if dy > 0 else pl.ds(0, 128)
            return remote(f.at[:, :, lanes], hyr.at[side], hss.at[n], hrs.at[back], device)
        return remote(cs.at[n], cr.at[back], hss.at[n], hrs.at[back], device)

    @pl.when(is_flow)
    def _():
        for c in range(3):
            for side, rows in ((0, 14), (1, 0)):
                for part in range(4):
                    hxs[side, c, 2 * part:2 * part + 2, :] = f[c, rows:rows + 2, 512 * part:512 * part + 512]
        for n, (dx, dy) in enumerate(DIRS):
            if dx and dy:
                rows, lanes = (14 if dx > 0 else 0), (1920 if dy > 0 else 0)
                for c in range(3):
                    cs[n, 2 * c:2 * c + 2, :] = f[c, rows:rows + 2, lanes:lanes + 128]
        for n, (dx, dy) in enumerate(DIRS):
            @pl.when(inside(dx, dy))
            def _():
                halo_copy(n).start()

    rotation = 3 * gx + 12 * gy

    def each_piece(body):
        def step(i, carry):
            o = (i + rotation) % 48
            k, q = o // 16, o % 16
            osec, ogx, ogy = owner_of(k, q)
            mine = (osec == sec) & (ogx == gx) & (ogy == gy)
            body(o, k, q, (osec, ogx, ogy), mine)
            return carry

        lax.fori_loop(0, 48, step, 0)

    rows16, lanes128 = pl.ds(gx * 16, 16), pl.ds(gy * 128, 128)

    def send_pieces(t, target, recv):
        def body(o, k, q, device, mine):
            @pl.when(jnp.logical_not(mine))
            def _():
                remote(PB.at[t, k, q], target, pss.at[t, o], recv, device).start()

            @pl.when(mine)
            def _():
                pltpu.make_async_copy(PB.at[t, k, q], target, recv).start()

        each_piece(body)

    def drain_pieces(t, target, recv):
        def body(o, k, q, device, mine):
            @pl.when(jnp.logical_not(mine))
            def _():
                remote(PB.at[t, k, q], target, pss.at[t, o], recv, device).wait_send()

        each_piece(body)

    def planes_of(src, t):
        def body(k, carry):
            blocks = to_planes([src[k, :, 128 * g:128 * g + 128] for g in range(16)])
            for q in range(16):
                PB[t, k, q] = blocks[q]
            return carry

        lax.fori_loop(0, 3, body, 0)

    @pl.when(sec == 3)
    def _():
        planes_of(f, 0)
        send_pieces(0, A.at[rows16, lanes128], ars)

    def each_operator(body):
        for j in range(4):
            for k in range(3):
                osec, ogx, ogy = owner_of(k, gy * 4 + j)
                body(0, 3 * j + k, k, (osec == sec), (ogx == gx), (sec, ogx, gy))
                osec, ogx, ogy = owner_of(k, 4 * j + gx % 4)
                body(1, 3 * j + k, k, (osec == sec) & (ogx == gx), (gy == j), (sec, gx, j))

    def operator_copies(kind, n, k):
        if kind == 0:
            return (
                (xo.at[:, k], X.at[:, rows16], xss.at[n], xrs),
                (cyl, CY.at[rows16], css.at[n], crs),
            )
        return (
            (yo.at[:, k], Y.at[:, pl.ds(gy * 64, 64)], yss.at[n], yrs),
            (cxl, CX.at[:, lanes128], dss.at[n], drs),
        )

    def start_operator(kind, n, k, wanted, mine, device):
        @pl.when(wanted & jnp.logical_not(mine))
        def _():
            for src, dst, ss, rs in operator_copies(kind, n, k):
                remote(src, dst, ss, rs, device).start()

        @pl.when(wanted & mine)
        def _():
            for src, dst, ss, rs in operator_copies(kind, n, k):
                pltpu.make_async_copy(src, dst, rs).start()

    def drain_operator(kind, n, k, wanted, mine, device):
        @pl.when(wanted & jnp.logical_not(mine))
        def _():
            for src, dst, ss, rs in operator_copies(kind, n, k):
                remote(src, dst, ss, rs, device).wait_send()

    @pl.when(sec % 2 == 1)
    def _():
        each_operator(start_operator)

    lane = lax.broadcasted_iota(jnp.int32, (24, 128), 1)
    row = lax.broadcasted_iota(jnp.int32, (24, 128), 0)

    def mixed(lamb, k):
        return coup[k, 0] * lamb[0] + coup[k, 1] * lamb[1] + coup[k, 2] * lamb[2]

    def tile_rows(value):
        return roll(value, -2, 0)[:16]

    @pl.when(is_flow)
    def _():
        U[...] = jnp.zeros_like(U)
        for c in range(3):
            for g in range(16):
                U[c, 2:18, 256 + 128 * g:384 + 128 * g] = f[c, :, 128 * g:128 * g + 128]
        for n, (dx, dy) in enumerate(DIRS):
            rows = {-1: 0, 0: 2, 1: 18}[dx]
            lanes = {-1: 128, 0: 256, 1: 2304}[dy]

            @pl.when(inside(dx, dy))
            def _():
                if dy == 0:
                    side = 0 if dx < 0 else 1
                    pltpu.make_async_copy(hxr.at[side], hxr.at[side], hrs.at[n]).wait()
                    for c in range(3):
                        for part in range(4):
                            U[c, rows:rows + 2, lanes + 512 * part:lanes + 512 * part + 512] = hxr[side, c, 2 * part:2 * part + 2, :]
                elif dx == 0:
                    side = 0 if dy < 0 else 1
                    pltpu.make_async_copy(hyr.at[side], hyr.at[side], hrs.at[n]).wait()
                    for c in range(3):
                        U[c, 2:18, lanes:lanes + 128] = hyr[side, c]
                else:
                    pltpu.make_async_copy(cr.at[n], cr.at[n], hrs.at[n]).wait()
                    for c in range(3):
                        U[c, rows:rows + 2, lanes:lanes + 128] = cr[n, 2 * c:2 * c + 2, :]

        V[...] = jnp.zeros_like(V)
        valid = ((row >= 2) | (gx > 0)) & ((row < 18) | (gx < 15))

        def edge(j, there):
            updated, _ = flow_block(U, j, lane)
            for c in range(3):
                V[c, :, 128 * j:128 * j + 128] = jnp.where(valid & there, updated[c], 0.0)

        edge(1, gy > 0)
        edge(18, gy < 3)

        def first(j, carry):
            updated, lamb = flow_block(U, j, lane)
            for c in range(3):
                V[c, :, pl.ds(pl.multiple_of(j * 128, 128), 128)] = jnp.where(valid, updated[c], 0.0)
                M[c, :, pl.ds(pl.multiple_of((j - 2) * 128, 128), 128)] = tile_rows(mixed(lamb, c))
            return carry

        lax.fori_loop(2, 18, first, 0)
        planes_of(M, 0)
        send_pieces(0, L.at[0, sec, rows16, lanes128], lrs.at[0])

        def second(j, carry):
            updated, lamb = flow_block(V, j, lane)
            for c in range(3):
                at = pl.ds(pl.multiple_of((j - 2) * 128, 128), 128)
                out[c, :, at] = tile_rows(updated[c])
                M[c, :, at] = tile_rows(mixed(lamb, c))
            return carry

        lax.fori_loop(2, 18, second, 0)
        planes_of(M, 1)
        send_pieces(1, L.at[1, sec, rows16, lanes128], lrs.at[1])

    @pl.when(is_owner)
    def _():
        i = lax.broadcasted_iota(jnp.int32, (256, 256), 0)
        j = lax.broadcasted_iota(jnp.int32, (256, 256), 1)
        for s in range(3):
            d = i - j - off[s, 0]
            SX[s] = jnp.where((d == 0) | (d == 1), 0.5, 0.0).astype(BF16)
            d = j - i - off[s, 1]
            SY[s] = jnp.where((d == 0) | (d == 1), 0.5, 0.0).astype(BF16)
        for ref, sem in ((X, xrs), (Y, yrs), (CY, crs), (CX, drs)):
            pltpu.make_async_copy(ref, ref, sem).wait()
        for c in range(NCLASS):
            high, low = split(X[c])
            XH[:, 256 * c:256 * c + 256] = high
            XL[:, 256 * c:256 * c + 256] = low
            high, low = split(Y[c].T)
            YH[256 * c:256 * c + 256, :] = high
            YL[256 * c:256 * c + 256, :] = low

        def separated(ref):
            a0, b0 = pair_swap(ref[:, 0:128], ref[:, 128:256])
            a1, b1 = pair_swap(ref[:, 256:384], ref[:, 384:512])
            return jnp.concatenate([a0, a1], axis=1), jnp.concatenate([b0, b1], axis=1)

        column_class = separated(CX)[0][0:1, :]
        column_class = jnp.concatenate([column_class, column_class], axis=1)
        row_class = CY[:, 0:1]

        def add_source(t):
            for s in range(3):
                for z, plane in enumerate(separated(L.at[t, s])):
                    high, low = split(plane)
                    shifted = dot(high, SY[s]) + dot(low, SY[s])
                    high, low = split(shifted)
                    TH[256 * s:256 * s + 256, 256 * z:256 * z + 256] = high
                    TL[256 * s:256 * s + 256, 256 * z:256 * z + 256] = low
            total = R[...]
            for s in range(3):
                total += dot(SX[s], TH[256 * s:256 * s + 256, :]) + dot(SX[s], TL[256 * s:256 * s + 256, :])
            return total

        def sweeps(value):
            high, low = split(value)
            for c in range(NCLASS):
                keep = column_class == c
                AH[256 * c:256 * c + 256, :] = jnp.where(keep, high, jnp.zeros_like(high))
                AL[256 * c:256 * c + 256, :] = jnp.where(keep, low, jnp.zeros_like(low))
            swept = dot(XH[...], AH[...]) + dot(XL[...], AH[...]) + dot(XH[...], AL[...])
            high, low = split(swept)
            for c in range(NCLASS):
                keep = row_class == c
                for z in range(2):
                    part_h, part_l = high[:, 256 * z:256 * z + 256], low[:, 256 * z:256 * z + 256]
                    BH[256 * z:256 * z + 256, 256 * c:256 * c + 256] = jnp.where(keep, part_h, jnp.zeros_like(part_h))
                    BL[256 * z:256 * z + 256, 256 * c:256 * c + 256] = jnp.where(keep, part_l, jnp.zeros_like(part_l))
            return dot(BH[...], YH[...]) + dot(BL[...], YH[...]) + dot(BH[...], YL[...])

        pltpu.make_async_copy(A, A, ars).wait()
        p0, p1 = separated(A)
        R[:, 0:256], R[:, 256:512] = p0, p1
        pltpu.make_async_copy(L.at[0], L.at[0], lrs.at[0]).wait()
        result = sweeps(add_source(0))
        R[:, 0:256], R[:, 256:512] = result[0:256], result[256:512]
        pltpu.make_async_copy(L.at[1], L.at[1], lrs.at[1]).wait()
        result = sweeps(add_source(1))
        for h in range(2):
            a, b = pair_swap(result[0:256, 128 * h:128 * h + 128], result[256:512, 128 * h:128 * h + 128])
            R[:, 256 * h:256 * h + 128] = a
            R[:, 256 * h + 128:256 * h + 256] = b

        def back(n):
            tx, ty = n % 16, n // 16
            mine = (sec == 3) & (tx == gx) & (ty == gy)
            src = R.at[pl.ds(pl.multiple_of(tx * 16, 16), 16), pl.ds(pl.multiple_of(ty * 128, 128), 128)]
            return mine, src, Q.at[my_k, my_q], (3, tx, ty)

        def give(i, carry):
            n = (i + rotation) % 64
            mine, src, dst, device = back(n)

            @pl.when(jnp.logical_not(mine))
            def _():
                remote(src, dst, rss.at[n], rrs, device).start()

            @pl.when(mine)
            def _():
                pltpu.make_async_copy(src, dst, rrs).start()

            return carry

        lax.fori_loop(0, 64, give, 0)

        def drain(n, carry):
            mine, src, dst, device = back(n)

            @pl.when(jnp.logical_not(mine))
            def _():
                remote(src, dst, rss.at[n], rrs, device).wait_send()

            return carry

        lax.fori_loop(0, 64, drain, 0)

    @pl.when(sec == 3)
    def _():
        pltpu.make_async_copy(Q, Q, rrs).wait()

        def body(k, carry):
            blocks = from_planes([Q[k, q] for q in range(16)])
            for g in range(16):
                out[k, :, 128 * g:128 * g + 128] = blocks[g]
            return carry

        lax.fori_loop(0, 3, body, 0)
        drain_pieces(0, A.at[rows16, lanes128], ars)

    @pl.when(sec % 2 == 1)
    def _():
        each_operator(drain_operator)

    @pl.when(is_flow)
    def _():
        for n, (dx, dy) in enumerate(DIRS):
            @pl.when(inside(dx, dy))
            def _():
                halo_copy(n).wait_send()
        for t in range(2):
            drain_pieces(t, L.at[t, sec, rows16, lanes128], lrs.at[t])


def local(fields, x_ops, y_ops, x_line_class, y_line_class, box_offset, coupling):
    member = jnp.minimum(lax.axis_index("sec"), 2)
    matrix = time_step * lax.dynamic_index_in_dim(coupling, member, 0, keepdims=False)
    row_class = jnp.broadcast_to(y_line_class.astype(F32)[:, None], (16, 128))
    column_class = jnp.broadcast_to(jnp.tile(x_line_class.astype(F32), 2)[None, :], (8, 128))
    vmem, smem, any_space = (pl.BlockSpec(memory_space=m) for m in (pltpu.VMEM, pltpu.SMEM, pl.ANY))
    V, D = pltpu.VMEM, pltpu.SemaphoreType.DMA
    out = pl.pallas_call(
        kernel,
        out_shape=jax.ShapeDtypeStruct((3, 16, 2048), F32),
        in_specs=[smem, smem, vmem, any_space, any_space, vmem, vmem],
        out_specs=vmem,
        scratch_shapes=[
            V((3, 24, 2560), F32), V((3, 24, 2560), F32), V((3, 16, 2048), F32),
            V((2, 3, 8, 512), F32), V((2, 3, 8, 512), F32), V((2, 3, 16, 128), F32),
            V((8, 8, 128), F32), V((8, 8, 128), F32),
            V((2, 3, 16, 16, 128), F32), V((256, 512), F32), V((2, 3, 256, 512), F32),
            V((4, 256, 256), F32), V((4, 256, 256), F32), V((256, 128), F32), V((8, 512), F32),
            V((256, 512), F32), V((3, 16, 16, 128), F32),
            V((256, 1024), BF16), V((256, 1024), BF16), V((1024, 256), BF16), V((1024, 256), BF16),
            V((3, 256, 256), BF16), V((3, 256, 256), BF16), V((768, 512), BF16), V((768, 512), BF16),
            V((1024, 512), BF16), V((1024, 512), BF16), V((512, 1024), BF16), V((512, 1024), BF16),
            D((8,)), D((8,)), D((2, 48)), D, D((2,)),
            D((12,)), D((12,)), D((12,)), D((12,)), D, D, D, D, D((64,)), D,
        ],
        compiler_params=pltpu.CompilerParams(has_side_effects=True, vmem_limit_bytes=60 << 20),
    )(matrix, box_offset, fields[0], x_ops, y_ops, row_class, column_class)
    return out[None]


def solution(mesh):
    placed = (
        P("sec", None, "gx", "gy"),
        P(None, None, "gx", None),
        P(None, None, "gy", None),
        P("gy"),
        P("gx"),
        P(),
        P(),
    )
    return jax.shard_map(
        local, mesh=mesh, in_specs=placed, out_specs=P("sec", None, "gx", "gy"), check_vma=False
    )
```

time: 705 us -> 89 us (0.13); the launches traced: 696 us -> 88.4 us
  waiting for transfers between devices: 544 us -> 0 us
  Pallas kernels: 0 us -> 82.1 us
  matrix products: 62.1 us -> 0 us
  starting transfers between devices: 37.1 us -> 0 us
  local copies, waits for them, and re-layouts: 24.3 us -> 5.02 us
  between operations: 16.6 us -> 0.02 us
  other arithmetic: 10.8 us -> 1.28 us
    all_gather x4 -> x0, waiting for transfers between devices: 303 us -> none  [the longest x2 157 us: sweep_lines_x(): lax.all_gather(state, 'gx', axis=2, tiled=True)]
    psum x2 -> x0, waiting for transfers between devices: 156 us -> none  [local(): source = lax.psum(contribution, 'sec')]
    ppermute x12 -> x0, waiting for transfers between devices: 85.2 us -> none  [the longest x4 79.7 us: shifted(): lax.ppermute(value, axis, [(source, source + steps) for source in range(i...]
    pallas_call x0 -> x1, Pallas kernels: none -> 82.1 us  [local(): pl.pallas_call(kernel, out_shape=jax.ShapeDtypeStruct((3, 16, 2048), F32)...]
    dot_general x6 -> x0, matrix products: 62.1 us -> none  [the longest x2 43.8 us: work(): jnp.einsum('ckij,kxjz->ckxiz', y_ops, portion[0], precision=highest)]
    ppermute x12 -> x0, starting transfers between devices: 36.7 us -> none  [the longest x4 13.1 us: padded_2(): lax.ppermute(lax.slice_in_dim(block, block.shape[dim] - width, None, axis...]
    reshape x5 -> x0, local copies, waits for them, and re-layouts: 7.93 us -> none  [the longest x2 3.5 us: local(): swept_x.reshape(1, 3, span_x, span_y, planes)]
  transfers between devices with their start and end apart: 18 -> 0, of which waited for: 14 -> 0; matrix products, arithmetic and copies ran while one was open for 1% -> 0% of each run, Pallas kernels for 0% -> 0%
where the time goes in v1:
time: 89 us; the launch traced here: 88.4 us
  Pallas kernels  82.1 us (92%)
  local copies, waits for them, and re-layouts  5.02 us (6%)
  other arithmetic  1.28 us (1%)
    pallas_call x1, Pallas kernels, local(): pl.pallas_call(kernel, out_shape=jax.ShapeDtypeStruct((3, 16, 2048), F32)...  82.1 us
    unnamed x8, local copies, waits for them, and re-layouts  3.67 us

profile of v1, /device:TPU:161, one launch (start us, length us, event | category | flops | bytes accessed | tf_op | source)
XLA Modules:
  0.0 88.4 jit_solution(14283271689995276185)
XLA Ops:
  0.0 0.0 copy-start.1
  0.0 0.7 copy-done.1
  0.7 0.0 copy-start.2
  0.7 0.1 broadcast_in_dim.17
  0.8 0.6 copy-done.2
  1.3 0.0 copy-start
  1.3 1.3 %multiply_bitcast_fusion.coup = f32[3,3]{1,0:T(4,128)} fusion(f32[3,3,3]{2,1,0:T(4,128)} %param.13, s32[]{:T(128)S(6)} %select_n.4), kind=kLoop, calls=%fused_computation | loop fusion | flops 9 | bytes 76 | tf_op jit(solution)/shard_map/mul | solution.py:452
  2.6 0.0 copy-done
  2.6 0.7 copy.8.off
  3.3 0.6 broadcast_in_dim.18.cxl
  3.9 0.7 broadcast_in_dim.16.cyl
  4.5 82.1 %shard_map.73 = f32[3,16,2048]{2,1,0:T(8,128)} custom-call(f32[3,3]{1,0:T(4,128)} %multiply_bitcast_fusion.coup, s32[3,2]{1,0:T(4,128)} %copy.8.off, f32[3,16,2048]{2,1,0:T(8,128)} %bitcast.5, f32[4,3,16,256]{3,2,1,0:T(8,128)} %xo.1, f32[4,3,64,256]{3,2,1,0:T(8,128)} %yo.1, f32[16,128]{1,0:T(8,128)} %broadcast_in_dim.16.cyl, f32[8,128]{1,0:T(8,128)} %broadcast_in_dim.18.cxl), custom_call_target="tpu_custom_call" | custom-call | tf_op jit(solution)/shard_map/pallas_call | solution.py:457
  86.7 1.8 %copy.10 = f32[1,3,16,2048]{3,2,1,0:T(8,128)} copy(f32[1,3,16,2048]{3,2,1,0:T(8,128)} %bitcast.4) | data formatting | bytes 786432
  (3 shorter events, 0.0 us)
Async XLA Ops:
  0.0 0.7 copy-start.1
  0.7 0.7 copy-start.2
  1.3 1.3 %copy-start = (s32[3,2]{0,1:T(2,128)S(1)}, s32[3,2]{0,1:T(2,128)}, u32[]{:S(2)}) copy-start(s32[3,2]{0,1:T(2,128)} %param.12) | copy-start | bytes 76

commit v2 on v1

v2 whole, which is shorter than its diff:
```python
import functools

import jax
import jax.numpy as jnp
from jax import lax
from jax.experimental import pallas as pl
from jax.experimental.pallas import tpu as pltpu
from jax.sharding import PartitionSpec as P

CZ = 32
NCLASS = 4
time_step = 0.2
viscosity = 0.25
MESH = pl.DeviceIdType.MESH
F32 = jnp.float32
BF16 = jnp.bfloat16

DIRS = [(dx, dy) for dx in (-1, 0, 1) for dy in (-1, 0, 1) if (dx, dy) != (0, 0)]


def div(a, b):
    return lax.div(a, jnp.int32(b))


def rem(a, b):
    return lax.rem(a, jnp.int32(b))


def device_at(x, y, z, core):
    return 2 * div(z, 4) + core, rem(z, 4) * 4 + y, x


def owner_of(m, q):
    z = m + (m >= 4).astype(jnp.int32)
    return device_at(div(q, 4), rem(q, 4), z, 1)


def roll(value, shift, axis):
    size = value.shape[axis]
    shift = shift % size
    return value if shift == 0 else pltpu.roll(value, shift, axis)


def lanes_of(value):
    return lax.broadcasted_iota(jnp.int32, value.shape, value.ndim - 1)


def swap_blocks(blocks):
    lane = lanes_of(blocks[0])
    blocks = list(blocks)
    for bit in (3, 2, 1, 0):
        d, width = 1 << bit, 2 << bit
        upper = (lane & width) != 0
        for i in range(16):
            if i & d:
                continue
            a, b = blocks[i], blocks[i | d]
            blocks[i] = jnp.where(upper, roll(b, width, 1), a)
            blocks[i | d] = jnp.where(upper, b, roll(a, -width, 1))
    return blocks


def take_lanes(value, index):
    return jnp.take_along_axis(value, index, axis=1, mode="promise_in_bounds")


def to_planes(blocks):
    lane = lanes_of(blocks[0])
    rest = lane % 64
    index = (rest % 4) * 32 + (rest // 4) * 2 + lane // 64
    return [take_lanes(b, index) for b in swap_blocks(blocks)]


def from_planes(blocks):
    lane = lanes_of(blocks[0])
    index = (lane % 2) * 64 + ((lane % 32) // 2) * 4 + lane // 32
    return swap_blocks([take_lanes(b, index) for b in blocks])


def pair_swap(a, b):
    upper = lanes_of(a) >= 64
    return jnp.where(upper, roll(b, 64, 1), a), jnp.where(upper, b, roll(a, 64, 1))


def split(value):
    high = value.astype(BF16)
    return high, (value - high.astype(F32)).astype(BF16)


def dot(a, b):
    return lax.dot_general(a, b, (((1,), (0,)), ((), ())), preferred_element_type=F32)


def flow_block(ref, j, lane):
    def block(c, at):
        return ref[c, :, pl.ds(pl.multiple_of(at * 128, 128), 128)]

    z = lane % CZ
    centre, ax, bx, ay, by, az, bz = [], [], [], [], [], [], []
    for c in range(3):
        cur, prv, nxt = block(c, j), block(c, j - 1), block(c, j + 1)
        centre.append(cur)
        ax.append(roll(cur, -1, 0))
        bx.append(roll(cur, 1, 0))
        ay.append(jnp.where(lane < 96, roll(cur, -32, 1), roll(nxt, -32, 1)))
        by.append(jnp.where(lane >= 32, roll(cur, 32, 1), roll(prv, 32, 1)))
        az.append(jnp.where(z != CZ - 1, roll(cur, -1, 1), roll(cur, 31, 1)))
        bz.append(jnp.where(z != 0, roll(cur, 1, 1), roll(cur, -31, 1)))
    omega_x = 0.5 * ((ay[2] - by[2]) - (az[1] - bz[1]))
    omega_y = 0.5 * ((az[0] - bz[0]) - (ax[2] - bx[2]))
    omega_z = 0.5 * ((ax[1] - bx[1]) - (ay[0] - by[0]))
    u, v, w = centre
    lamb = [omega_y * w - omega_z * v, omega_z * u - omega_x * w, omega_x * v - omega_y * u]
    updated = []
    for c in range(3):
        laplace = ax[c] + bx[c] + ay[c] + by[c] + az[c] + bz[c] - 6.0 * centre[c]
        updated.append(centre[c] + time_step * (viscosity * laplace - lamb[c]))
    return updated, lamb


def kernel(
    coup, off, f, xo, yo, xcls, ycls, out,
    U, V, M, hxs, hxr, hyr, cs, cr, PB, A, L, X, Y, CY, CX, CYL, CXL, R, D, Q,
    XH, XL, YH, YL, SX, SY, TH, TL, AH, AL, BH, BL,
    hss, hrs, pss, ars, lrs, xss, yss, css, dss, xrs, yrs, crs, drs, rss, rrs, known_x, known_y,
):
    sec, gx, gy = lax.axis_index("sec"), lax.axis_index("gx"), lax.axis_index("gy")
    x, y, z, core = gy, rem(gx, 4), 4 * div(sec, 2) + div(gx, 4), rem(sec, 2)
    is_flow = sec < 3
    is_owner = (core == 1) & (z != 4) & (z != 7)
    my_q = 4 * x + y
    my_m = z - (z > 4).astype(jnp.int32)
    my_o = my_m * 16 + my_q

    def remote(src, dst, ss, rs, device):
        return pltpu.make_async_remote_copy(
            src_ref=src, dst_ref=dst, send_sem=ss, recv_sem=rs, device_id=device, device_id_type=MESH
        )

    def wait_for(ref, sem):
        pltpu.make_async_copy(ref, ref, sem).wait()

    def signal(sem, device):
        pl.semaphore_signal(sem, inc=1, device_id=device, device_id_type=MESH)

    barrier = pltpu.get_barrier_semaphore()
    greeted = 0
    for dx, dy in DIRS:
        signal(barrier, (sec, rem(gx + dx + 16, 16), rem(gy + dy + 4, 4)))
        greeted += 1
    signal(barrier, device_at(rem(x + 2, 4), y, z, core))
    for d in (1, 2, 3):
        signal(barrier, device_at(x, rem(y + d, 4), z, core))
    signal(barrier, device_at(x, y, z, 1 - core))
    for d in range(1, 8):
        for c in range(2):
            signal(barrier, device_at(x, y, rem(z + d, 8), c))
    greeted += 1 + 3 + 1 + 14

    def inside(dx, dy):
        return (gx + dx >= 0) & (gx + dx < 16) & (gy + dy >= 0) & (gy + dy < 4)

    @pl.when(is_flow)
    def _():
        for c in range(3):
            for side, rows in ((0, 14), (1, 0)):
                for part in range(4):
                    hxs[side, c, 2 * part:2 * part + 2, :] = f[c, rows:rows + 2, 512 * part:512 * part + 512]
        for n, (dx, dy) in enumerate(DIRS):
            if dx and dy:
                rows, lanes = (14 if dx > 0 else 0), (1920 if dy > 0 else 0)
                for c in range(3):
                    cs[n, 2 * c:2 * c + 2, :] = f[c, rows:rows + 2, lanes:lanes + 128]
        U[...] = jnp.zeros_like(U)
        for c in range(3):
            for g in range(16):
                U[c, 2:18, 256 + 128 * g:384 + 128 * g] = f[c, :, 128 * g:128 * g + 128]
        for c in range(3):
            for j in (0, 1, 18, 19):
                V[c, :, 128 * j:128 * j + 128] = jnp.zeros((24, 128), F32)

    @pl.when(core == 1)
    def _():
        CXL[...] = jnp.zeros_like(CXL)
        CXL[:, 0:64] = jnp.broadcast_to(xcls[...].astype(F32), (8, 64))
        spread = jnp.broadcast_to(ycls[...].astype(F32), (16, 16))
        diagonal = lax.broadcasted_iota(jnp.int32, (16, 16), 0) == lax.broadcasted_iota(jnp.int32, (16, 16), 1)
        column = jnp.sum(jnp.where(diagonal, spread, 0.0), axis=1, keepdims=True)
        CYL[...] = jnp.broadcast_to(column, (16, 128))

    pl.semaphore_wait(barrier, greeted)

    def halo_copy(n):
        dx, dy = DIRS[n]
        back = DIRS.index((-dx, -dy))
        device = (sec, gx + dx, gy + dy)
        if dy == 0:
            side = 0 if dx > 0 else 1
            return remote(hxs.at[side], hxr.at[side], hss.at[n], hrs.at[back], device)
        if dx == 0:
            side = 0 if dy > 0 else 1
            lanes = pl.ds(1920, 128) if dy > 0 else pl.ds(0, 128)
            return remote(f.at[:, :, lanes], hyr.at[side], hss.at[n], hrs.at[back], device)
        return remote(cs.at[n], cr.at[back], hss.at[n], hrs.at[back], device)

    @pl.when(is_flow)
    def _():
        for n, (dx, dy) in enumerate(DIRS):
            @pl.when(inside(dx, dy))
            def _():
                halo_copy(n).start()

    for d in (1, 2, 3):
        signal(known_x, device_at(rem(x + d, 4), y, z, core))

    rotation = 16 * rem(z, 6) + my_q
    rows8, rows16, lanes128 = pl.ds(gx * 8, 8), pl.ds(gx * 16, 16), pl.ds(gy * 128, 128)

    def send_pieces(t, target, recv):
        def step(i, carry):
            o = i + rotation
            o = jnp.where(o >= 96, o - 96, o)
            device = owner_of(div(o, 16), rem(o, 16))
            mine = is_owner & (o == my_o)

            @pl.when(jnp.logical_not(mine))
            def _():
                remote(PB.at[t, o], target, pss.at[t], recv, device).start()

            @pl.when(mine)
            def _():
                pltpu.make_async_copy(PB.at[t, o], target, recv).start()

            return carry

        lax.fori_loop(0, 96, step, 0)

    def drain_pieces(t):
        @pl.when(is_owner)
        def _():
            wait_for(PB.at[t, pl.ds(0, 95)], pss.at[t])

        @pl.when(jnp.logical_not(is_owner))
        def _():
            wait_for(PB.at[t], pss.at[t])

    def planes_of(src, t):
        def body(k, carry):
            blocks = to_planes([src[k, :, 128 * g:128 * g + 128] for g in range(16)])
            for q in range(16):
                even, odd = pair_swap(blocks[q][0:8], blocks[q][8:16])
                PB[t, 32 * k + q] = even
                PB[t, 32 * k + 16 + q] = odd
            return carry

        lax.fori_loop(0, 3, body, 0)

    def each_operator(body):
        for dz in (-2, -1, 0, 1, 2):
            oz = rem(z + dz + 8, 8)
            k = div(oz - (oz > 4).astype(jnp.int32), 2)
            holds = (oz != 4) & (oz != 7)
            for j in range(4):
                wanted = holds
                if dz in (-2, 2):
                    wanted = holds & (rem(x + j, 2) == (0 if dz < 0 else 1))
                mine = (y == j) if dz == 0 else None
                body(0, 4 * (dz + 2) + j, k, wanted, mine, device_at(x, j, oz, 1))
        for j in range(4):
            body(1, j, div(my_m, 2), is_owner, x == j, device_at(j, y, z, 1))

    def operator_copies(kind, n, k):
        if kind == 0:
            return (
                (xo.at[:, k], X.at[:, rows16], xss.at[n], xrs),
                (CYL, CY.at[rows16], css.at[n], crs),
            )
        return (
            (yo.at[:, k], Y.at[:, pl.ds(gy * 64, 64)], yss.at[n], yrs),
            (CXL, CX.at[:, lanes128], dss.at[n], drs),
        )

    def start_operator(kind, n, k, wanted, mine, device):
        far = wanted if mine is None else wanted & jnp.logical_not(mine)

        @pl.when(far)
        def _():
            for src, dst, ss, rs in operator_copies(kind, n, k):
                remote(src, dst, ss, rs, device).start()

        if mine is not None:
            @pl.when(wanted & mine)
            def _():
                for src, dst, ss, rs in operator_copies(kind, n, k):
                    pltpu.make_async_copy(src, dst, rs).start()

    def drain_operator(kind, n, k, wanted, mine, device):
        far = wanted if mine is None else wanted & jnp.logical_not(mine)

        @pl.when(far)
        def _():
            for src, dst, ss, rs in operator_copies(kind, n, k):
                remote(src, dst, ss, rs, device).wait_send()

    @pl.when(sec == 3)
    def _():
        planes_of(f, 0)

    pl.semaphore_wait(known_x, 3)
    for d in (1, 2, 3):
        signal(known_y, device_at(x, rem(y + d, 4), z, core))

    lane = lax.broadcasted_iota(jnp.int32, (24, 128), 1)
    row = lax.broadcasted_iota(jnp.int32, (24, 128), 0)

    def mixed(lamb, k):
        at = jnp.minimum(sec, 2)
        total = coup[at, k, 0] * lamb[0] + coup[at, k, 1] * lamb[1] + coup[at, k, 2] * lamb[2]
        return time_step * total

    def tile_rows(value):
        return roll(value, -2, 0)[:16]

    @pl.when(is_flow)
    def _():
        for n, (dx, dy) in enumerate(DIRS):
            rows = {-1: 0, 0: 2, 1: 18}[dx]
            lanes = {-1: 128, 0: 256, 1: 2304}[dy]

            @pl.when(inside(dx, dy))
            def _():
                if dy == 0:
                    side = 0 if dx < 0 else 1
                    wait_for(hxr.at[side], hrs.at[n])
                    for c in range(3):
                        for part in range(4):
                            U[c, rows:rows + 2, lanes + 512 * part:lanes + 512 * part + 512] = hxr[side, c, 2 * part:2 * part + 2, :]
                elif dx == 0:
                    side = 0 if dy < 0 else 1
                    wait_for(hyr.at[side], hrs.at[n])
                    for c in range(3):
                        U[c, 2:18, lanes:lanes + 128] = hyr[side, c]
                else:
                    wait_for(cr.at[n], hrs.at[n])
                    for c in range(3):
                        U[c, rows:rows + 2, lanes:lanes + 128] = cr[n, 2 * c:2 * c + 2, :]

    pl.semaphore_wait(known_y, 3)

    @pl.when(core == 1)
    def _():
        each_operator(start_operator)

    @pl.when(sec == 3)
    def _():
        send_pieces(0, A.at[rows8, lanes128], ars)

    @pl.when(is_flow)
    def _():
        valid = ((row >= 2) | (gx > 0)) & ((row < 18) | (gx < 15))

        def edge(j, there):
            updated, _ = flow_block(U, j, lane)
            for c in range(3):
                V[c, :, 128 * j:128 * j + 128] = jnp.where(valid & there, updated[c], 0.0)

        def first(j, carry):
            updated, lamb = flow_block(U, j, lane)
            for c in range(3):
                V[c, :, pl.ds(pl.multiple_of(j * 128, 128), 128)] = jnp.where(valid, updated[c], 0.0)
                M[c, :, pl.ds(pl.multiple_of((j - 2) * 128, 128), 128)] = tile_rows(mixed(lamb, c))
            return carry

        lax.fori_loop(2, 18, first, 0)
        planes_of(M, 0)
        send_pieces(0, L.at[0, sec, rows8, lanes128], lrs.at[0])
        edge(1, gy > 0)
        edge(18, gy < 3)

        def second(j, carry):
            updated, lamb = flow_block(V, j, lane)
            for c in range(3):
                at = pl.ds(pl.multiple_of((j - 2) * 128, 128), 128)
                out[c, :, at] = tile_rows(updated[c])
                M[c, :, at] = tile_rows(mixed(lamb, c))
            return carry

        lax.fori_loop(2, 18, second, 0)
        planes_of(M, 1)
        send_pieces(1, L.at[1, sec, rows8, lanes128], lrs.at[1])

    @pl.when(is_owner)
    def _():
        i = lax.broadcasted_iota(jnp.int32, (256, 256), 0)
        j = lax.broadcasted_iota(jnp.int32, (256, 256), 1)
        for s in range(3):
            d = i - j - off[0, s]
            SX[:, 256 * s:256 * s + 256] = jnp.where((d == 0) | (d == 1), 0.5, 0.0).astype(BF16)
            d = j - i - off[1, s]
            SY[s] = jnp.where((d == 0) | (d == 1), 0.5, 0.0).astype(BF16)
        for ref, sem in ((X, xrs), (Y, yrs), (CY, crs), (CX, drs)):
            wait_for(ref, sem)
        for c in range(NCLASS):
            high, low = split(X[c])
            XH[:, 256 * c:256 * c + 256] = high
            XL[:, 256 * c:256 * c + 256] = low
            high, low = split(Y[c].T)
            YH[256 * c:256 * c + 256, :] = high
            YL[256 * c:256 * c + 256, :] = low

        def unpacked(ref):
            halves = []
            for h in range(2):
                a, b = pair_swap(ref[:, 256 * h:256 * h + 128], ref[:, 256 * h + 128:256 * h + 256])
                rows = jnp.stack([a.reshape(16, 8, 128), b.reshape(16, 8, 128)], axis=1)
                halves.append(rows.reshape(256, 128))
            return jnp.concatenate(halves, axis=1)

        column_class = jnp.concatenate(
            [pair_swap(CX[:, 256 * h:256 * h + 128], CX[:, 256 * h + 128:256 * h + 256])[0][0:1] for h in range(2)], axis=1
        )
        row_class = CY[:, 0:1]

        def add_source(t):
            for s in range(3):
                high, low = split(unpacked(L.at[t, s]))
                high, low = split(dot(high, SY[s]) + dot(low, SY[s]))
                TH[256 * s:256 * s + 256, :] = high
                TL[256 * s:256 * s + 256, :] = low
            return D[...] + dot(SX[...], TH[...]) + dot(SX[...], TL[...])

        def sweeps(value):
            high, low = split(value)
            for c in range(NCLASS):
                keep = column_class == c
                AH[256 * c:256 * c + 256, :] = jnp.where(keep, high, jnp.zeros_like(high))
                AL[256 * c:256 * c + 256, :] = jnp.where(keep, low, jnp.zeros_like(low))
            swept = dot(XH[...], AH[...]) + dot(XL[...], AH[...]) + dot(XH[...], AL[...])
            high, low = split(swept)
            for c in range(NCLASS):
                keep = row_class == c
                BH[:, 256 * c:256 * c + 256] = jnp.where(keep, high, jnp.zeros_like(high))
                BL[:, 256 * c:256 * c + 256] = jnp.where(keep, low, jnp.zeros_like(low))
            return dot(BH[...], YH[...]) + dot(BL[...], YH[...]) + dot(BH[...], YL[...])

        wait_for(A, ars)
        D[...] = unpacked(A)
        wait_for(L.at[0], lrs.at[0])
        D[...] = sweeps(add_source(0))
        wait_for(L.at[1], lrs.at[1])
        result = sweeps(add_source(1))
        for h in range(2):
            rows = result[:, 128 * h:128 * h + 128].reshape(16, 2, 8, 128)
            a, b = pair_swap(rows[:, 0].reshape(128, 128), rows[:, 1].reshape(128, 128))
            R[:, 256 * h:256 * h + 128] = a
            R[:, 256 * h + 128:256 * h + 256] = b

        def give(i, carry):
            n = i + 16 * y + 4 * x + rem(z, 4)
            n = jnp.where(n >= 64, n - 64, n)
            tx, ty = div(n, 4), rem(n, 4)
            mine = (sec == 3) & (tx == gx) & (ty == gy)
            src = R.at[pl.ds(pl.multiple_of(tx * 8, 8), 8), pl.ds(pl.multiple_of(ty * 128, 128), 128)]

            @pl.when(jnp.logical_not(mine))
            def _():
                remote(src, Q.at[my_o], rss, rrs, (3, tx, ty)).start()

            @pl.when(mine)
            def _():
                pltpu.make_async_copy(src, Q.at[my_o], rrs).start()

            return carry

        lax.fori_loop(0, 64, give, 0)

    @pl.when(sec == 3)
    def _():
        wait_for(Q, rrs)

        def body(k, carry):
            blocks = []
            for q in range(16):
                a, b = pair_swap(Q[32 * k + q], Q[32 * k + 16 + q])
                blocks.append(jnp.concatenate([a, b], axis=0))
            blocks = from_planes(blocks)
            for g in range(16):
                out[k, :, 128 * g:128 * g + 128] = blocks[g]
            return carry

        lax.fori_loop(0, 3, body, 0)
        drain_pieces(0)

    @pl.when(is_owner & (sec == 3))
    def _():
        wait_for(Q.at[pl.ds(0, 63)], rss)

    @pl.when(is_owner & (sec != 3))
    def _():
        wait_for(Q.at[pl.ds(0, 64)], rss)

    @pl.when(core == 1)
    def _():
        each_operator(drain_operator)

    @pl.when(is_flow)
    def _():
        for n, (dx, dy) in enumerate(DIRS):
            @pl.when(inside(dx, dy))
            def _():
                halo_copy(n).wait_send()
        for t in range(2):
            drain_pieces(t)


def local(fields, x_ops, y_ops, x_line_class, y_line_class, box_offset, coupling):
    vmem, smem, any_space = (pl.BlockSpec(memory_space=m) for m in (pltpu.VMEM, pltpu.SMEM, pl.ANY))
    V, D = pltpu.VMEM, pltpu.SemaphoreType.DMA
    out = pl.pallas_call(
        kernel,
        out_shape=jax.ShapeDtypeStruct((3, 16, 2048), F32),
        in_specs=[smem, smem, vmem, any_space, any_space, vmem, vmem],
        out_specs=vmem,
        scratch_shapes=[
            V((3, 24, 2560), F32), V((3, 24, 2560), F32), V((3, 16, 2048), F32),
            V((2, 3, 8, 512), F32), V((2, 3, 8, 512), F32), V((2, 3, 16, 128), F32),
            V((8, 8, 128), F32), V((8, 8, 128), F32),
            V((2, 96, 8, 128), F32), V((128, 512), F32), V((2, 3, 128, 512), F32),
            V((4, 256, 256), F32), V((4, 256, 256), F32), V((256, 128), F32), V((8, 512), F32),
            V((16, 128), F32), V((8, 128), F32),
            V((128, 512), F32), V((256, 256), F32), V((96, 8, 128), F32),
            V((256, 1024), BF16), V((256, 1024), BF16), V((1024, 256), BF16), V((1024, 256), BF16),
            V((256, 768), BF16), V((3, 256, 256), BF16), V((768, 256), BF16), V((768, 256), BF16),
            V((1024, 256), BF16), V((1024, 256), BF16), V((256, 1024), BF16), V((256, 1024), BF16),
            D((8,)), D((8,)), D((2,)), D, D((2,)),
            D((20,)), D((4,)), D((20,)), D((4,)), D, D, D, D, D, D,
            pltpu.SemaphoreType.REGULAR, pltpu.SemaphoreType.REGULAR,
        ],
        compiler_params=pltpu.CompilerParams(
            collective_id=0, has_side_effects=True, vmem_limit_bytes=60 << 20
        ),
    )(coupling, box_offset.T, fields[0], x_ops, y_ops, x_line_class[None], y_line_class[None])
    return out[None]


def solution(mesh):
    placed = (
        P("sec", None, "gx", "gy"),
        P(None, None, "gx", None),
        P(None, None, "gy", None),
        P("gy"),
        P("gx"),
        P(),
        P(),
    )
    return jax.shard_map(
        local, mesh=mesh, in_specs=placed, out_specs=P("sec", None, "gx", "gy"), check_vma=False
    )
```

time: 89 us -> 58.4 us (0.66)
  Pallas kernels: 82.1 us -> 56.3 us
  local copies, waits for them, and re-layouts: 5.02 us -> 1.77 us
  other arithmetic: 1.28 us -> 0 us
    pallas_call x1, Pallas kernels: 82.1 us -> 56.3 us  [local(): pl.pallas_call(kernel, out_shape=jax.ShapeDtypeStruct((3, 16, 2048), F32)...]
    unnamed x8 -> x1, local copies, waits for them, and re-layouts: 3.67 us -> 1.77 us
    broadcast_in_dim x3 -> x0, local copies, waits for them, and re-layouts: 1.35 us -> none  [the longest x2 0.68 us: local(): jnp.broadcast_to(jnp.tile(x_line_class.astype(F32), 2)[None, :], (8, 128))]
    mul x1 -> x0, other arithmetic: 1.28 us -> none  [local(): time_step * lax.dynamic_index_in_dim(coupling, member, 0, keepdims=False)]
where the time goes in v2:
time: 58.4 us; the launch traced here: 58 us
  Pallas kernels  56.3 us (96%)
  local copies, waits for them, and re-layouts  1.77 us (3%)
    pallas_call x1, Pallas kernels, local(): pl.pallas_call(kernel, out_shape=jax.ShapeDtypeStruct((3, 16, 2048), F32)...  56.3 us
    unnamed x1, local copies, waits for them, and re-layouts  1.77 us

profile of v2, /device:TPU:161, one launch (start us, length us, event | category | flops | bytes accessed | tf_op | source)
XLA Modules:
  0.0 58.0 jit_solution(4698919371992946455)
XLA Ops:
  0.0 56.3 %shard_map.73 = f32[3,16,2048]{2,1,0:T(8,128)} custom-call(f32[3,3,3]{2,1,0:T(4,128)} %coup.1, s32[2,3]{1,0:T(2,128)} %bitcast.7, f32[3,16,2048]{2,1,0:T(8,128)} %bitcast.6, f32[4,3,16,256]{3,2,1,0:T(8,128)} %xo.1, f32[4,3,64,256]{3,2,1,0:T(8,128)} %yo.1, s32[1,64]{1,0:T(1,128)} %bitcast.8, s32[1,16]{1,0:T(1,128)} %bitcast.9), custom_call_target="tpu_custom_call" | custom-call | tf_op jit(solution)/shard_map/pallas_call | solution.py:519
  56.3 1.8 %copy.9 = f32[1,3,16,2048]{3,2,1,0:T(8,128)} copy(f32[1,3,16,2048]{3,2,1,0:T(8,128)} %bitcast.5) | data formatting | bytes 786432

commit v3 on v2

--- a/solution.py
+++ b/solution.py
@@ -30,9 +30,8 @@
     return 2 * div(z, 4) + core, rem(z, 4) * 4 + y, x
 
 
-def owner_of(m, q):
-    z = m + (m >= 4).astype(jnp.int32)
-    return device_at(div(q, 4), rem(q, 4), z, 1)
+def far_first():
+    return sorted(((dx, dy) for dx in range(4) for dy in range(4)), key=lambda d: -sum(min(v, 4 - v) for v in d))
 
 
 def roll(value, shift, axis):
@@ -91,19 +90,24 @@
     return lax.dot_general(a, b, (((1,), (0,)), ((), ())), preferred_element_type=F32)
 
 
-def flow_block(ref, j, lane):
-    def block(c, at):
-        return ref[c, :, pl.ds(pl.multiple_of(at * 128, 128), 128)]
-
+def flow_block(ref, j, lane, rows):
+    def block(c, at, first, count):
+        return ref[c, first:first + count, pl.ds(pl.multiple_of(at * 128, 128), 128)]
+
+    first, count = (0, 24) if rows is None else rows
     z = lane % CZ
     centre, ax, bx, ay, by, az, bz = [], [], [], [], [], [], []
     for c in range(3):
-        cur, prv, nxt = block(c, j), block(c, j - 1), block(c, j + 1)
+        cur, prv, nxt = (block(c, at, first, count) for at in (j, j - 1, j + 1))
         centre.append(cur)
-        ax.append(roll(cur, -1, 0))
-        bx.append(roll(cur, 1, 0))
-        ay.append(jnp.where(lane < 96, roll(cur, -32, 1), roll(nxt, -32, 1)))
-        by.append(jnp.where(lane >= 32, roll(cur, 32, 1), roll(prv, 32, 1)))
+        if rows is None:
+            ax.append(roll(cur, -1, 0))
+            bx.append(roll(cur, 1, 0))
+        else:
+            ax.append(block(c, j, first + 1, count))
+            bx.append(block(c, j, first - 1, count))
+        ay.append(roll(jnp.where(lane < 32, nxt, cur), -32, 1))
+        by.append(roll(jnp.where(lane < 96, cur, prv), 32, 1))
         az.append(jnp.where(z != CZ - 1, roll(cur, -1, 1), roll(cur, 31, 1)))
         bz.append(jnp.where(z != 0, roll(cur, 1, 1), roll(cur, -31, 1)))
     omega_x = 0.5 * ((ay[2] - by[2]) - (az[1] - bz[1]))
@@ -122,7 +126,7 @@
     coup, off, f, xo, yo, xcls, ycls, out,
     U, V, M, hxs, hxr, hyr, cs, cr, PB, A, L, X, Y, CY, CX, CYL, CXL, R, D, Q,
     XH, XL, YH, YL, SX, SY, TH, TL, AH, AL, BH, BL,
-    hss, hrs, pss, ars, lrs, xss, yss, css, dss, xrs, yrs, crs, drs, rss, rrs, known_x, known_y,
+    hss, hrs, pss, ars, lrs, xss, yss, css, dss, xrs, xrs2, yrs, crs, crs2, drs, rss, rrs, known_x, known_y,
 ):
     sec, gx, gy = lax.axis_index("sec"), lax.axis_index("gx"), lax.axis_index("gy")
     x, y, z, core = gy, rem(gx, 4), 4 * div(sec, 2) + div(gx, 4), rem(sec, 2)
@@ -177,7 +181,7 @@
                 U[c, 2:18, 256 + 128 * g:384 + 128 * g] = f[c, :, 128 * g:128 * g + 128]
         for c in range(3):
             for j in (0, 1, 18, 19):
-                V[c, :, 128 * j:128 * j + 128] = jnp.zeros((24, 128), F32)
+                V[c, :, 128 * j:128 * j + 128] = jnp.zeros((32, 128), F32)
 
     @pl.when(core == 1)
     def _():
@@ -210,30 +214,90 @@
             def _():
                 halo_copy(n).start()
 
+    lanes128 = pl.ds(gy * 128, 128)
+    my_zl = div(gx, 4)
+
+    def start(wanted, src, dst, ss, rs, device):
+        @pl.when(wanted)
+        def _():
+            remote(src, dst, ss, rs, device).start()
+
+    def start_here(wanted, src, dst, rs):
+        @pl.when(wanted)
+        def _():
+            pltpu.make_async_copy(src, dst, rs).start()
+
+    def drain(wanted, src, dst, ss, rs, device):
+        @pl.when(wanted)
+        def _():
+            remote(src, dst, ss, rs, device).wait_send()
+
+    def x_column(act):
+        for n, dz in enumerate((-1, 1, 2, -2)):
+            oz = rem(z + dz + 8, 8)
+            k = div(oz - (oz > 4).astype(jnp.int32), 2)
+            wanted = (core == 1) & (oz != 4) & (oz != 7)
+            if n >= 2:
+                wanted = wanted & (rem(x + y, 2) == n - 2)
+            act(wanted, xo.at[:, k], X.at[:, my_zl, y], xss.at[n], xrs, device_at(x, y, oz, 1))
+            act(wanted, CYL, CY.at[my_zl, y], css.at[n], crs, device_at(x, y, oz, 1))
+
+    def x_along(act):
+        for d in (1, 2, 3):
+            device = device_at(x, rem(y + d, 4), z, 1)
+            act(is_owner, X.at[:, :, y], X.at[:, :, y], xss.at[3 + d], xrs2, device)
+            act(is_owner, CY.at[:, y], CY.at[:, y], css.at[3 + d], crs2, device)
+
+    def y_along(act):
+        mine_y = pl.ds(gy * 64, 64)
+        for d in (1, 2, 3):
+            device = device_at(rem(x + d, 4), y, z, 1)
+            act(is_owner, yo.at[:, div(my_m, 2)], Y.at[:, mine_y], yss.at[d - 1], yrs, device)
+            act(is_owner, CXL, CX.at[:, lanes128], dss.at[d - 1], drs, device)
+
+    x_column(start)
+    y_along(start)
+    start_here(is_owner, xo.at[:, div(my_m, 2)], X.at[:, my_zl, y], xrs)
+    start_here(is_owner, CYL, CY.at[my_zl, y], crs)
+    start_here(is_owner, yo.at[:, div(my_m, 2)], Y.at[:, pl.ds(gy * 64, 64)], yrs)
+    start_here(is_owner, CXL, CX.at[:, lanes128], drs)
+
+    def forward_x():
+        @pl.when(is_owner)
+        def _():
+            wait_for(X.at[:, :, y], xrs)
+            wait_for(CY.at[:, y], crs)
+
+        x_along(start)
+
     for d in (1, 2, 3):
         signal(known_x, device_at(rem(x + d, 4), y, z, core))
 
-    rotation = 16 * rem(z, 6) + my_q
-    rows8, rows16, lanes128 = pl.ds(gx * 8, 8), pl.ds(gx * 16, 16), pl.ds(gy * 128, 128)
+    rows8 = pl.ds(gx * 8, 8)
 
     def send_pieces(t, target, recv):
-        def step(i, carry):
-            o = i + rotation
-            o = jnp.where(o >= 96, o - 96, o)
-            device = owner_of(div(o, 16), rem(o, 16))
-            mine = is_owner & (o == my_o)
-
-            @pl.when(jnp.logical_not(mine))
-            def _():
-                remote(PB.at[t, o], target, pss.at[t], recv, device).start()
-
-            @pl.when(mine)
-            def _():
-                pltpu.make_async_copy(PB.at[t, o], target, recv).start()
-
-            return carry
-
-        lax.fori_loop(0, 96, step, 0)
+        layers = []
+        for i in range(6):
+            m = rem(z + 3 + i, 6)
+            oz = m + (m >= 4).astype(jnp.int32)
+            layers.append((m * 16, 2 * div(oz, 4) + 1, rem(oz, 4) * 4, m))
+        for dx, dy in far_first():
+            tx, ty = rem(x + dx, 4), rem(y + dy, 4)
+            q = 4 * tx + ty
+            for base, osec, ogx, m in layers:
+                copy = remote(PB.at[t, base + q], target, pss.at[t], recv, (osec, ogx + ty, tx))
+                if dx or dy:
+                    copy.start()
+                    continue
+                mine = is_owner & (m == my_m)
+
+                @pl.when(jnp.logical_not(mine))
+                def _():
+                    copy.start()
+
+                @pl.when(mine)
+                def _():
+                    pltpu.make_async_copy(PB.at[t, base + q], target, recv).start()
 
     def drain_pieces(t):
         @pl.when(is_owner)
@@ -255,53 +319,6 @@
 
         lax.fori_loop(0, 3, body, 0)
 
-    def each_operator(body):
-        for dz in (-2, -1, 0, 1, 2):
-            oz = rem(z + dz + 8, 8)
-            k = div(oz - (oz > 4).astype(jnp.int32), 2)
-            holds = (oz != 4) & (oz != 7)
-            for j in range(4):
-                wanted = holds
-                if dz in (-2, 2):
-                    wanted = holds & (rem(x + j, 2) == (0 if dz < 0 else 1))
-                mine = (y == j) if dz == 0 else None
-                body(0, 4 * (dz + 2) + j, k, wanted, mine, device_at(x, j, oz, 1))
-        for j in range(4):
-            body(1, j, div(my_m, 2), is_owner, x == j, device_at(j, y, z, 1))
-
-    def operator_copies(kind, n, k):
-        if kind == 0:
-            return (
-                (xo.at[:, k], X.at[:, rows16], xss.at[n], xrs),
-                (CYL, CY.at[rows16], css.at[n], crs),
-            )
-        return (
-            (yo.at[:, k], Y.at[:, pl.ds(gy * 64, 64)], yss.at[n], yrs),
-            (CXL, CX.at[:, lanes128], dss.at[n], drs),
-        )
-
-    def start_operator(kind, n, k, wanted, mine, device):
-        far = wanted if mine is None else wanted & jnp.logical_not(mine)
-
-        @pl.when(far)
-        def _():
-            for src, dst, ss, rs in operator_copies(kind, n, k):
-                remote(src, dst, ss, rs, device).start()
-
-        if mine is not None:
-            @pl.when(wanted & mine)
-            def _():
-                for src, dst, ss, rs in operator_copies(kind, n, k):
-                    pltpu.make_async_copy(src, dst, rs).start()
-
-    def drain_operator(kind, n, k, wanted, mine, device):
-        far = wanted if mine is None else wanted & jnp.logical_not(mine)
-
-        @pl.when(far)
-        def _():
-            for src, dst, ss, rs in operator_copies(kind, n, k):
-                remote(src, dst, ss, rs, device).wait_send()
-
     @pl.when(sec == 3)
     def _():
         planes_of(f, 0)
@@ -317,9 +334,6 @@
         at = jnp.minimum(sec, 2)
         total = coup[at, k, 0] * lamb[0] + coup[at, k, 1] * lamb[1] + coup[at, k, 2] * lamb[2]
         return time_step * total
-
-    def tile_rows(value):
-        return roll(value, -2, 0)[:16]
 
     @pl.when(is_flow)
     def _():
@@ -345,47 +359,56 @@
                     for c in range(3):
                         U[c, rows:rows + 2, lanes:lanes + 128] = cr[n, 2 * c:2 * c + 2, :]
 
-    pl.semaphore_wait(known_y, 3)
-
-    @pl.when(core == 1)
-    def _():
-        each_operator(start_operator)
-
     @pl.when(sec == 3)
     def _():
+        pl.semaphore_wait(known_y, 3)
         send_pieces(0, A.at[rows8, lanes128], ars)
+        forward_x()
 
     @pl.when(is_flow)
     def _():
         valid = ((row >= 2) | (gx > 0)) & ((row < 18) | (gx < 15))
 
+        def keep(j, updated):
+            at = pl.ds(pl.multiple_of(j * 128, 128), 128)
+            for c in range(3):
+                rolled = roll(updated[c], -2, 0)
+                V[c, 8:24, at] = rolled[0:16]
+                V[c, 0:8, at] = rolled[16:24]
+                V[c, 24:32, at] = rolled[16:24]
+
         def edge(j, there):
-            updated, _ = flow_block(U, j, lane)
+            updated, _ = flow_block(U, j, lane, None)
+            keep(j, [jnp.where(valid & there, value, 0.0) for value in updated])
+
+        def first(j, carry):
+            updated, lamb = flow_block(U, j, lane, None)
+            keep(j, [jnp.where(valid, value, 0.0) for value in updated])
             for c in range(3):
-                V[c, :, 128 * j:128 * j + 128] = jnp.where(valid & there, updated[c], 0.0)
-
-        def first(j, carry):
-            updated, lamb = flow_block(U, j, lane)
-            for c in range(3):
-                V[c, :, pl.ds(pl.multiple_of(j * 128, 128), 128)] = jnp.where(valid, updated[c], 0.0)
-                M[c, :, pl.ds(pl.multiple_of((j - 2) * 128, 128), 128)] = tile_rows(mixed(lamb, c))
+                M[c, :, pl.ds(pl.multiple_of((j - 2) * 128, 128), 128)] = roll(mixed(lamb, c), -2, 0)[0:16]
             return carry
 
-        lax.fori_loop(2, 18, first, 0)
+        lax.fori_loop(2, 18, first, 0, unroll=2)
         planes_of(M, 0)
+        pl.semaphore_wait(known_y, 3)
         send_pieces(0, L.at[0, sec, rows8, lanes128], lrs.at[0])
+
+        @pl.when(core == 1)
+        def _():
+            forward_x()
+
         edge(1, gy > 0)
         edge(18, gy < 3)
 
         def second(j, carry):
-            updated, lamb = flow_block(V, j, lane)
+            updated, lamb = flow_block(V, j, lane[0:16], (8, 16))
             for c in range(3):
                 at = pl.ds(pl.multiple_of((j - 2) * 128, 128), 128)
-                out[c, :, at] = tile_rows(updated[c])
-                M[c, :, at] = tile_rows(mixed(lamb, c))
+                out[c, :, at] = updated[c]
+                M[c, :, at] = mixed(lamb, c)
             return carry
 
-        lax.fori_loop(2, 18, second, 0)
+        lax.fori_loop(2, 18, second, 0, unroll=2)
         planes_of(M, 1)
         send_pieces(1, L.at[1, sec, rows8, lanes128], lrs.at[1])
 
@@ -398,10 +421,12 @@
             SX[:, 256 * s:256 * s + 256] = jnp.where((d == 0) | (d == 1), 0.5, 0.0).astype(BF16)
             d = j - i - off[1, s]
             SY[s] = jnp.where((d == 0) | (d == 1), 0.5, 0.0).astype(BF16)
-        for ref, sem in ((X, xrs), (Y, yrs), (CY, crs), (CX, drs)):
-            wait_for(ref, sem)
+        wait_for(X.at[:, :, pl.ds(0, 3)], xrs2)
+        wait_for(CY.at[:, pl.ds(0, 3)], crs2)
+        wait_for(Y, yrs)
+        wait_for(CX, drs)
         for c in range(NCLASS):
-            high, low = split(X[c])
+            high, low = split(X[c].reshape(256, 256))
             XH[:, 256 * c:256 * c + 256] = high
             XL[:, 256 * c:256 * c + 256] = low
             high, low = split(Y[c].T)
@@ -419,7 +444,7 @@
         column_class = jnp.concatenate(
             [pair_swap(CX[:, 256 * h:256 * h + 128], CX[:, 256 * h + 128:256 * h + 256])[0][0:1] for h in range(2)], axis=1
         )
-        row_class = CY[:, 0:1]
+        row_class = CY[...].reshape(256, 128)[:, 0:1]
 
         def add_source(t):
             for s in range(3):
@@ -455,24 +480,25 @@
             R[:, 256 * h:256 * h + 128] = a
             R[:, 256 * h + 128:256 * h + 256] = b
 
-        def give(i, carry):
-            n = i + 16 * y + 4 * x + rem(z, 4)
-            n = jnp.where(n >= 64, n - 64, n)
-            tx, ty = div(n, 4), rem(n, 4)
-            mine = (sec == 3) & (tx == gx) & (ty == gy)
-            src = R.at[pl.ds(pl.multiple_of(tx * 8, 8), 8), pl.ds(pl.multiple_of(ty * 128, 128), 128)]
-
-            @pl.when(jnp.logical_not(mine))
-            def _():
-                remote(src, Q.at[my_o], rss, rrs, (3, tx, ty)).start()
-
-            @pl.when(mine)
-            def _():
-                pltpu.make_async_copy(src, Q.at[my_o], rrs).start()
-
-            return carry
-
-        lax.fori_loop(0, 64, give, 0)
+        for dx, dy in far_first():
+            tx, ty = rem(x + dx, 4), rem(y + dy, 4)
+            for i in range(4):
+                zl = rem(z + 2 + i, 4)
+                rows = pl.ds(pl.multiple_of((4 * zl + ty) * 8, 8), 8)
+                src = R.at[rows, pl.ds(pl.multiple_of(tx * 128, 128), 128)]
+                copy = remote(src, Q.at[my_o], rss, rrs, (3, 4 * zl + ty, tx))
+                if dx or dy:
+                    copy.start()
+                    continue
+                mine = (sec == 3) & (zl == my_zl)
+
+                @pl.when(jnp.logical_not(mine))
+                def _():
+                    copy.start()
+
+                @pl.when(mine)
+                def _():
+                    pltpu.make_async_copy(src, Q.at[my_o], rrs).start()
 
     @pl.when(sec == 3)
     def _():
@@ -499,9 +525,9 @@
     def _():
         wait_for(Q.at[pl.ds(0, 64)], rss)
 
-    @pl.when(core == 1)
-    def _():
-        each_operator(drain_operator)
+    x_column(drain)
+    x_along(drain)
+    y_along(drain)
 
     @pl.when(is_flow)
     def _():
@@ -522,18 +548,18 @@
         in_specs=[smem, smem, vmem, any_space, any_space, vmem, vmem],
         out_specs=vmem,
         scratch_shapes=[
-            V((3, 24, 2560), F32), V((3, 24, 2560), F32), V((3, 16, 2048), F32),
+            V((3, 24, 2560), F32), V((3, 32, 2560), F32), V((3, 16, 2048), F32),
             V((2, 3, 8, 512), F32), V((2, 3, 8, 512), F32), V((2, 3, 16, 128), F32),
             V((8, 8, 128), F32), V((8, 8, 128), F32),
             V((2, 96, 8, 128), F32), V((128, 512), F32), V((2, 3, 128, 512), F32),
-            V((4, 256, 256), F32), V((4, 256, 256), F32), V((256, 128), F32), V((8, 512), F32),
+            V((4, 4, 4, 16, 256), F32), V((4, 256, 256), F32), V((4, 4, 16, 128), F32), V((8, 512), F32),
             V((16, 128), F32), V((8, 128), F32),
             V((128, 512), F32), V((256, 256), F32), V((96, 8, 128), F32),
             V((256, 1024), BF16), V((256, 1024), BF16), V((1024, 256), BF16), V((1024, 256), BF16),
             V((256, 768), BF16), V((3, 256, 256), BF16), V((768, 256), BF16), V((768, 256), BF16),
             V((1024, 256), BF16), V((1024, 256), BF16), V((256, 1024), BF16), V((256, 1024), BF16),
             D((8,)), D((8,)), D((2,)), D, D((2,)),
-            D((20,)), D((4,)), D((20,)), D((4,)), D, D, D, D, D, D,
+            D((7,)), D((3,)), D((7,)), D((3,)), D, D, D, D, D, D, D, D,
             pltpu.SemaphoreType.REGULAR, pltpu.SemaphoreType.REGULAR,
         ],
         compiler_params=pltpu.CompilerParams(

time: 58.4 us -> 51.6 us (0.88)
  Pallas kernels: 56.3 us -> 49.7 us
    pallas_call x1, Pallas kernels: 56.3 us -> 49.7 us  [local(): pl.pallas_call(kernel, out_shape=jax.ShapeDtypeStruct((3, 16, 2048), F32)...]
where the time goes in v3:
time: 51.6 us; the launch traced here: 51.5 us
  Pallas kernels  49.7 us (96%)
  local copies, waits for them, and re-layouts  1.77 us (3%)
    pallas_call x1, Pallas kernels, local(): pl.pallas_call(kernel, out_shape=jax.ShapeDtypeStruct((3, 16, 2048), F32)...  49.7 us
    unnamed x1, local copies, waits for them, and re-layouts  1.77 us

profile of v3, /device:TPU:161, one launch (start us, length us, event | category | flops | bytes accessed | tf_op | source)
XLA Modules:
  0.0 51.5 jit_solution(13486666338103640169)
XLA Ops:
  0.0 49.7 %shard_map.73 = f32[3,16,2048]{2,1,0:T(8,128)} custom-call(f32[3,3,3]{2,1,0:T(4,128)} %coup.1, s32[2,3]{1,0:T(2,128)} %bitcast.7, f32[3,16,2048]{2,1,0:T(8,128)} %bitcast.6, f32[4,3,16,256]{3,2,1,0:T(8,128)} %xo.1, f32[4,3,64,256]{3,2,1,0:T(8,128)} %yo.1, s32[1,64]{1,0:T(1,128)} %bitcast.8, s32[1,16]{1,0:T(1,128)} %bitcast.9), custom_call_target="tpu_custom_call" | custom-call | tf_op jit(solution)/shard_map/pallas_call | solution.py:545
  49.8 1.8 %copy.9 = f32[1,3,16,2048]{3,2,1,0:T(8,128)} copy(f32[1,3,16,2048]{3,2,1,0:T(8,128)} %bitcast.5) | data formatting | bytes 786432

commit v4 on v3

--- a/solution.py
+++ b/solution.py
@@ -54,8 +54,9 @@
             if i & d:
                 continue
             a, b = blocks[i], blocks[i | d]
-            blocks[i] = jnp.where(upper, roll(b, width, 1), a)
-            blocks[i | d] = jnp.where(upper, b, roll(a, -width, 1))
+            crossing = take_lanes(jnp.where(upper, a, b), lane ^ width)
+            blocks[i] = jnp.where(upper, crossing, a)
+            blocks[i | d] = jnp.where(upper, b, crossing)
     return blocks
 
 
@@ -78,7 +79,8 @@
 
 def pair_swap(a, b):
     upper = lanes_of(a) >= 64
-    return jnp.where(upper, roll(b, 64, 1), a), jnp.where(upper, b, roll(a, 64, 1))
+    crossing = roll(jnp.where(upper, a, b), 64, 1)
+    return jnp.where(upper, crossing, a), jnp.where(upper, b, crossing)
 
 
 def split(value):
@@ -126,7 +128,7 @@
     coup, off, f, xo, yo, xcls, ycls, out,
     U, V, M, hxs, hxr, hyr, cs, cr, PB, A, L, X, Y, CY, CX, CYL, CXL, R, D, Q,
     XH, XL, YH, YL, SX, SY, TH, TL, AH, AL, BH, BL,
-    hss, hrs, pss, ars, lrs, xss, yss, css, dss, xrs, xrs2, yrs, crs, crs2, drs, rss, rrs, known_x, known_y,
+    hss, hrs, pss, ars, lrs, xss, yss, css, dss, xrs, xrs2, yrs, crs, crs2, drs, rss, rrs, known_z, known_x, known_y,
 ):
     sec, gx, gy = lax.axis_index("sec"), lax.axis_index("gx"), lax.axis_index("gy")
     x, y, z, core = gy, rem(gx, 4), 4 * div(sec, 2) + div(gx, 4), rem(sec, 2)
@@ -148,21 +150,24 @@
         pl.semaphore_signal(sem, inc=1, device_id=device, device_id_type=MESH)
 
     barrier = pltpu.get_barrier_semaphore()
+
+    def inside(dx, dy):
+        return (gx + dx >= 0) & (gx + dx < 16) & (gy + dy >= 0) & (gy + dy < 4)
+
     greeted = 0
     for dx, dy in DIRS:
-        signal(barrier, (sec, rem(gx + dx + 16, 16), rem(gy + dy + 4, 4)))
-        greeted += 1
-    signal(barrier, device_at(rem(x + 2, 4), y, z, core))
+        @pl.when(inside(dx, dy))
+        def _():
+            signal(barrier, (sec, gx + dx, gy + dy))
+        greeted += inside(dx, dy).astype(jnp.int32)
     for d in (1, 2, 3):
+        signal(barrier, device_at(rem(x + d, 4), y, z, core))
         signal(barrier, device_at(x, rem(y + d, 4), z, core))
     signal(barrier, device_at(x, y, z, 1 - core))
-    for d in range(1, 8):
+    for d in (-2, -1, 1, 2):
         for c in range(2):
-            signal(barrier, device_at(x, y, rem(z + d, 8), c))
-    greeted += 1 + 3 + 1 + 14
-
-    def inside(dx, dy):
-        return (gx + dx >= 0) & (gx + dx < 16) & (gy + dy >= 0) & (gy + dy < 4)
+            signal(barrier, device_at(x, y, rem(z + d + 8, 8), c))
+    greeted += 6 + 1 + 8
 
     @pl.when(is_flow)
     def _():
@@ -270,62 +275,60 @@
 
         x_along(start)
 
-    for d in (1, 2, 3):
-        signal(known_x, device_at(rem(x + d, 4), y, z, core))
+    for d in (-2, -1, 1, 2):
+        signal(known_z, device_at(x, y, rem(z + d + 8, 8), core))
 
     rows8 = pl.ds(gx * 8, 8)
 
-    def send_pieces(t, target, recv):
-        layers = []
-        for i in range(6):
-            m = rem(z + 3 + i, 6)
-            oz = m + (m >= 4).astype(jnp.int32)
-            layers.append((m * 16, 2 * div(oz, 4) + 1, rem(oz, 4) * 4, m))
-        for dx, dy in far_first():
-            tx, ty = rem(x + dx, 4), rem(y + dy, 4)
-            q = 4 * tx + ty
-            for base, osec, ogx, m in layers:
-                copy = remote(PB.at[t, base + q], target, pss.at[t], recv, (osec, ogx + ty, tx))
-                if dx or dy:
-                    copy.start()
-                    continue
-                mine = is_owner & (m == my_m)
-
-                @pl.when(jnp.logical_not(mine))
-                def _():
-                    copy.start()
-
-                @pl.when(mine)
-                def _():
-                    pltpu.make_async_copy(PB.at[t, base + q], target, recv).start()
-
-    def drain_pieces(t):
-        @pl.when(is_owner)
-        def _():
-            wait_for(PB.at[t, pl.ds(0, 95)], pss.at[t])
-
-        @pl.when(jnp.logical_not(is_owner))
-        def _():
-            wait_for(PB.at[t], pss.at[t])
-
-    def planes_of(src, t):
-        def body(k, carry):
+    def send_planes(src, t, target, recv, ready):
+        first_k = rem(div(z, 2) + 1, 3)
+        for i in range(3):
+            k = rem(first_k + i, 3)
             blocks = to_planes([src[k, :, 128 * g:128 * g + 128] for g in range(16)])
             for q in range(16):
                 even, odd = pair_swap(blocks[q][0:8], blocks[q][8:16])
                 PB[t, 32 * k + q] = even
                 PB[t, 32 * k + 16 + q] = odd
-            return carry
-
-        lax.fori_loop(0, 3, body, 0)
-
-    @pl.when(sec == 3)
-    def _():
-        planes_of(f, 0)
-
-    pl.semaphore_wait(known_x, 3)
+            if i == 0:
+                ready()
+            layers = []
+            for parity in range(2):
+                m = 2 * k + parity
+                oz = m + (m >= 4).astype(jnp.int32)
+                layers.append((m * 16, 2 * div(oz, 4) + 1, rem(oz, 4) * 4, m))
+            for dx, dy in far_first():
+                tx, ty = rem(x + dx, 4), rem(y + dy, 4)
+                q = 4 * tx + ty
+                for base, osec, ogx, m in layers:
+                    copy = remote(PB.at[t, base + q], target, pss.at[t], recv, (osec, ogx + ty, tx))
+                    if dx or dy:
+                        copy.start()
+                        continue
+                    mine = is_owner & (m == my_m)
+
+                    @pl.when(jnp.logical_not(mine))
+                    def _():
+                        copy.start()
+
+                    @pl.when(mine)
+                    def _():
+                        pltpu.make_async_copy(PB.at[t, base + q], target, recv).start()
+
+    def everyone():
+        pl.semaphore_wait(known_y, 3)
+
+    def drain_pieces(t):
+        @pl.when(is_owner)
+        def _():
+            wait_for(PB.at[t, pl.ds(0, 95)], pss.at[t])
+
+        @pl.when(jnp.logical_not(is_owner))
+        def _():
+            wait_for(PB.at[t], pss.at[t])
+
+    pl.semaphore_wait(known_z, 4)
     for d in (1, 2, 3):
-        signal(known_y, device_at(x, rem(y + d, 4), z, core))
+        signal(known_x, device_at(rem(x + d, 4), y, z, core))
 
     lane = lax.broadcasted_iota(jnp.int32, (24, 128), 1)
     row = lax.broadcasted_iota(jnp.int32, (24, 128), 0)
@@ -359,10 +362,13 @@
                     for c in range(3):
                         U[c, rows:rows + 2, lanes:lanes + 128] = cr[n, 2 * c:2 * c + 2, :]
 
+    pl.semaphore_wait(known_x, 3)
+    for d in (1, 2, 3):
+        signal(known_y, device_at(x, rem(y + d, 4), z, core))
+
     @pl.when(sec == 3)
     def _():
-        pl.semaphore_wait(known_y, 3)
-        send_pieces(0, A.at[rows8, lanes128], ars)
+        send_planes(f, 0, A.at[rows8, lanes128], ars, everyone)
         forward_x()
 
     @pl.when(is_flow)
@@ -389,9 +395,7 @@
             return carry
 
         lax.fori_loop(2, 18, first, 0, unroll=2)
-        planes_of(M, 0)
-        pl.semaphore_wait(known_y, 3)
-        send_pieces(0, L.at[0, sec, rows8, lanes128], lrs.at[0])
+        send_planes(M, 0, L.at[0, sec, rows8, lanes128], lrs.at[0], everyone)
 
         @pl.when(core == 1)
         def _():
@@ -409,8 +413,7 @@
             return carry
 
         lax.fori_loop(2, 18, second, 0, unroll=2)
-        planes_of(M, 1)
-        send_pieces(1, L.at[1, sec, rows8, lanes128], lrs.at[1])
+        send_planes(M, 1, L.at[1, sec, rows8, lanes128], lrs.at[1], lambda: None)
 
     @pl.when(is_owner)
     def _():
@@ -560,7 +563,7 @@
             V((1024, 256), BF16), V((1024, 256), BF16), V((256, 1024), BF16), V((256, 1024), BF16),
             D((8,)), D((8,)), D((2,)), D, D((2,)),
             D((7,)), D((3,)), D((7,)), D((3,)), D, D, D, D, D, D, D, D,
-            pltpu.SemaphoreType.REGULAR, pltpu.SemaphoreType.REGULAR,
+            pltpu.SemaphoreType.REGULAR, pltpu.SemaphoreType.REGULAR, pltpu.SemaphoreType.REGULAR,
         ],
         compiler_params=pltpu.CompilerParams(
             collective_id=0, has_side_effects=True, vmem_limit_bytes=60 << 20

time: 51.6 us -> 51.2 us (level)
  Pallas kernels: 49.7 us -> 49.1 us
    pallas_call x1, Pallas kernels: 49.7 us -> 49.1 us  [local(): pl.pallas_call(kernel, out_shape=jax.ShapeDtypeStruct((3, 16, 2048), F32)...]
where the time goes in v4:
time: 51.2 us; the launch traced here: 50.8 us
  Pallas kernels  49.1 us (96%)
  local copies, waits for them, and re-layouts  1.77 us (3%)
    pallas_call x1, Pallas kernels, local(): pl.pallas_call(kernel, out_shape=jax.ShapeDtypeStruct((3, 16, 2048), F32)...  49.1 us
    unnamed x1, local copies, waits for them, and re-layouts  1.77 us

profile of v4, /device:TPU:161, one launch (start us, length us, event | category | flops | bytes accessed | tf_op | source)
XLA Modules:
  0.0 50.8 jit_solution(11550976085109175835)
XLA Ops:
  0.0 49.1 %shard_map.73 = f32[3,16,2048]{2,1,0:T(8,128)} custom-call(f32[3,3,3]{2,1,0:T(4,128)} %coup.1, s32[2,3]{1,0:T(2,128)} %bitcast.7, f32[3,16,2048]{2,1,0:T(8,128)} %bitcast.6, f32[4,3,16,256]{3,2,1,0:T(8,128)} %xo.1, f32[4,3,64,256]{3,2,1,0:T(8,128)} %yo.1, s32[1,64]{1,0:T(1,128)} %bitcast.8, s32[1,16]{1,0:T(1,128)} %bitcast.9), custom_call_target="tpu_custom_call" | custom-call | tf_op jit(solution)/shard_map/pallas_call | solution.py:548
  49.1 1.8 %copy.9 = f32[1,3,16,2048]{3,2,1,0:T(8,128)} copy(f32[1,3,16,2048]{3,2,1,0:T(8,128)} %bitcast.5) | data formatting | bytes 786432

commit v5 on v4

--- a/solution.py
+++ b/solution.py
@@ -9,6 +9,7 @@
 
 CZ = 32
 NCLASS = 4
+PARTS = 1
 time_step = 0.2
 viscosity = 0.25
 MESH = pl.DeviceIdType.MESH
@@ -125,15 +126,16 @@
 
 
 def kernel(
-    coup, off, f, xo, yo, xcls, ycls, out,
-    U, V, M, hxs, hxr, hyr, cs, cr, PB, A, L, X, Y, CY, CX, CYL, CXL, R, D, Q,
-    XH, XL, YH, YL, SX, SY, TH, TL, AH, AL, BH, BL,
-    hss, hrs, pss, ars, lrs, xss, yss, css, dss, xrs, xrs2, yrs, crs, crs2, drs, rss, rrs, known_z, known_x, known_y,
+    coup, off, fields, xo, yo, xcls, ycls, out,
+    f, U, V, M, hxs, hxr, hyr, cs, cr, PB, A, L, X, Y, CY, CX, CYL, CXL, R, D, Q,
+    XHH, XL, YHH, YL, SX, SY, TT, AA, BB,
+    load, hss, hrs, pss, ars, lrs, xss, yss, css, dss, xrs, xrs2, yrs, crs, crs2, drs, rss, rrs, known_x, known_y,
 ):
     sec, gx, gy = lax.axis_index("sec"), lax.axis_index("gx"), lax.axis_index("gy")
     x, y, z, core = gy, rem(gx, 4), 4 * div(sec, 2) + div(gx, 4), rem(sec, 2)
     is_flow = sec < 3
     is_owner = (core == 1) & (z != 4) & (z != 7)
+    is_helper = (core == 0) & (z != 4) & (z != 7)
     my_q = 4 * x + y
     my_m = z - (z > 4).astype(jnp.int32)
     my_o = my_m * 16 + my_q
@@ -161,13 +163,36 @@
             signal(barrier, (sec, gx + dx, gy + dy))
         greeted += inside(dx, dy).astype(jnp.int32)
     for d in (1, 2, 3):
-        signal(barrier, device_at(rem(x + d, 4), y, z, core))
+        signal(barrier, device_at(rem(x + d, 4), y, z, 0))
+        signal(barrier, device_at(rem(x + d, 4), y, z, 1))
         signal(barrier, device_at(x, rem(y + d, 4), z, core))
     signal(barrier, device_at(x, y, z, 1 - core))
-    for d in (-2, -1, 1, 2):
+    for d in range(1, 8):
         for c in range(2):
-            signal(barrier, device_at(x, y, rem(z + d + 8, 8), c))
-    greeted += 6 + 1 + 8
+            signal(barrier, device_at(x, y, rem(z + d, 8), c))
+    greeted += 9 + 1 + 14
+    loading = pltpu.make_async_copy(fields, f, load)
+    loading.start()
+
+    CXL[...] = jnp.zeros_like(CXL)
+    CXL[:, 0:64] = jnp.broadcast_to(xcls[...].astype(F32), (8, 64))
+    spread = jnp.broadcast_to(ycls[...].astype(F32), (16, 16))
+    diagonal = lax.broadcasted_iota(jnp.int32, (16, 16), 0) == lax.broadcasted_iota(jnp.int32, (16, 16), 1)
+    column = jnp.sum(jnp.where(diagonal, spread, 0.0), axis=1, keepdims=True)
+    CYL[...] = jnp.broadcast_to(column, (16, 128))
+
+    def relay_planes(src, t, k):
+        blocks = to_planes([src[k, :, 128 * g:128 * g + 128] for g in range(16)])
+        for q in range(16):
+            even, odd = pair_swap(blocks[q][0:8], blocks[q][8:16])
+            PB[t, 32 * k + q] = even
+            PB[t, 32 * k + 16 + q] = odd
+
+    loading.wait()
+
+    @pl.when(sec == 3)
+    def _():
+        lax.fori_loop(0, 3, lambda k, carry: (relay_planes(f, 0, k), carry)[1], 0)
 
     @pl.when(is_flow)
     def _():
@@ -180,24 +205,11 @@
                 rows, lanes = (14 if dx > 0 else 0), (1920 if dy > 0 else 0)
                 for c in range(3):
                     cs[n, 2 * c:2 * c + 2, :] = f[c, rows:rows + 2, lanes:lanes + 128]
-        U[...] = jnp.zeros_like(U)
-        for c in range(3):
-            for g in range(16):
-                U[c, 2:18, 256 + 128 * g:384 + 128 * g] = f[c, :, 128 * g:128 * g + 128]
-        for c in range(3):
-            for j in (0, 1, 18, 19):
-                V[c, :, 128 * j:128 * j + 128] = jnp.zeros((32, 128), F32)
-
-    @pl.when(core == 1)
-    def _():
-        CXL[...] = jnp.zeros_like(CXL)
-        CXL[:, 0:64] = jnp.broadcast_to(xcls[...].astype(F32), (8, 64))
-        spread = jnp.broadcast_to(ycls[...].astype(F32), (16, 16))
-        diagonal = lax.broadcasted_iota(jnp.int32, (16, 16), 0) == lax.broadcasted_iota(jnp.int32, (16, 16), 1)
-        column = jnp.sum(jnp.where(diagonal, spread, 0.0), axis=1, keepdims=True)
-        CYL[...] = jnp.broadcast_to(column, (16, 128))
 
     pl.semaphore_wait(barrier, greeted)
+
+    for d in (1, 2, 3):
+        signal(known_x, device_at(rem(x + d, 4), y, z, core))
 
     def halo_copy(n):
         dx, dy = DIRS[n]
@@ -257,8 +269,8 @@
         mine_y = pl.ds(gy * 64, 64)
         for d in (1, 2, 3):
             device = device_at(rem(x + d, 4), y, z, 1)
-            act(is_owner, yo.at[:, div(my_m, 2)], Y.at[:, mine_y], yss.at[d - 1], yrs, device)
-            act(is_owner, CXL, CX.at[:, lanes128], dss.at[d - 1], drs, device)
+            act(is_helper, yo.at[:, div(my_m, 2)], Y.at[:, mine_y], yss.at[d - 1], yrs, device)
+            act(is_helper, CXL, CX.at[:, lanes128], dss.at[d - 1], drs, device)
 
     x_column(start)
     y_along(start)
@@ -275,8 +287,19 @@
 
         x_along(start)
 
-    for d in (-2, -1, 1, 2):
-        signal(known_z, device_at(x, y, rem(z + d + 8, 8), core))
+    @pl.when(is_flow)
+    def _():
+        U[...] = jnp.zeros_like(U)
+        for c in range(3):
+            for g in range(16):
+                U[c, 2:18, 256 + 128 * g:384 + 128 * g] = f[c, :, 128 * g:128 * g + 128]
+        for c in range(3):
+            for j in (0, 1, 18, 19):
+                V[c, :, 128 * j:128 * j + 128] = jnp.zeros((32, 128), F32)
+
+    pl.semaphore_wait(known_x, 3)
+    for d in (1, 2, 3):
+        signal(known_y, device_at(x, rem(y + d, 4), z, core))
 
     rows8 = pl.ds(gx * 8, 8)
 
@@ -284,11 +307,8 @@
         first_k = rem(div(z, 2) + 1, 3)
         for i in range(3):
             k = rem(first_k + i, 3)
-            blocks = to_planes([src[k, :, 128 * g:128 * g + 128] for g in range(16)])
-            for q in range(16):
-                even, odd = pair_swap(blocks[q][0:8], blocks[q][8:16])
-                PB[t, 32 * k + q] = even
-                PB[t, 32 * k + 16 + q] = odd
+            if src is not None:
+                relay_planes(src, t, k)
             if i == 0:
                 ready()
             layers = []
@@ -325,10 +345,6 @@
         @pl.when(jnp.logical_not(is_owner))
         def _():
             wait_for(PB.at[t], pss.at[t])
-
-    pl.semaphore_wait(known_z, 4)
-    for d in (1, 2, 3):
-        signal(known_x, device_at(rem(x + d, 4), y, z, core))
 
     lane = lax.broadcasted_iota(jnp.int32, (24, 128), 1)
     row = lax.broadcasted_iota(jnp.int32, (24, 128), 0)
@@ -362,14 +378,10 @@
                     for c in range(3):
                         U[c, rows:rows + 2, lanes:lanes + 128] = cr[n, 2 * c:2 * c + 2, :]
 
-    pl.semaphore_wait(known_x, 3)
-    for d in (1, 2, 3):
-        signal(known_y, device_at(x, rem(y + d, 4), z, core))
-
     @pl.when(sec == 3)
     def _():
-        send_planes(f, 0, A.at[rows8, lanes128], ars, everyone)
         forward_x()
+        send_planes(None, 0, A.at[my_zl, y, :, lanes128], ars, everyone)
 
     @pl.when(is_flow)
     def _():
@@ -395,11 +407,8 @@
             return carry
 
         lax.fori_loop(2, 18, first, 0, unroll=2)
-        send_planes(M, 0, L.at[0, sec, rows8, lanes128], lrs.at[0], everyone)
-
-        @pl.when(core == 1)
-        def _():
-            forward_x()
+        forward_x()
+        send_planes(M, 0, L.at[0, sec, rows8, lanes128], lrs.at[0, sec], everyone)
 
         edge(1, gy > 0)
         edge(18, gy < 3)
@@ -413,7 +422,7 @@
             return carry
 
         lax.fori_loop(2, 18, second, 0, unroll=2)
-        send_planes(M, 1, L.at[1, sec, rows8, lanes128], lrs.at[1], lambda: None)
+        send_planes(M, 1, L.at[1, sec, rows8, lanes128], lrs.at[1, sec], lambda: None)
 
     @pl.when(is_owner)
     def _():
@@ -421,19 +430,25 @@
         j = lax.broadcasted_iota(jnp.int32, (256, 256), 1)
         for s in range(3):
             d = i - j - off[0, s]
-            SX[:, 256 * s:256 * s + 256] = jnp.where((d == 0) | (d == 1), 0.5, 0.0).astype(BF16)
+            shift = jnp.where((d == 0) | (d == 1), 0.5, 0.0).astype(BF16)
+            SX[:, 256 * s:256 * s + 256] = shift
+            SX[:, 768 + 256 * s:1024 + 256 * s] = shift
             d = j - i - off[1, s]
-            SY[s] = jnp.where((d == 0) | (d == 1), 0.5, 0.0).astype(BF16)
+            shift = jnp.where((d == 0) | (d == 1), 0.5, 0.0).astype(BF16)
+            SY[s, 0:256] = shift
+            SY[s, 256:512] = shift
         wait_for(X.at[:, :, pl.ds(0, 3)], xrs2)
         wait_for(CY.at[:, pl.ds(0, 3)], crs2)
         wait_for(Y, yrs)
         wait_for(CX, drs)
         for c in range(NCLASS):
             high, low = split(X[c].reshape(256, 256))
-            XH[:, 256 * c:256 * c + 256] = high
+            XHH[:, 256 * c:256 * c + 256] = high
+            XHH[:, 1024 + 256 * c:1280 + 256 * c] = high
             XL[:, 256 * c:256 * c + 256] = low
             high, low = split(Y[c].T)
-            YH[256 * c:256 * c + 256, :] = high
+            YHH[256 * c:256 * c + 256, :] = high
+            YHH[1024 + 256 * c:1280 + 256 * c, :] = high
             YL[256 * c:256 * c + 256, :] = low
 
         def unpacked(ref):
@@ -450,65 +465,69 @@
         row_class = CY[...].reshape(256, 128)[:, 0:1]
 
         def add_source(t):
+            for s in (2, 0, 1):
+                wait_for(L.at[t, s], lrs.at[t, s])
             for s in range(3):
                 high, low = split(unpacked(L.at[t, s]))
-                high, low = split(dot(high, SY[s]) + dot(low, SY[s]))
-                TH[256 * s:256 * s + 256, :] = high
-                TL[256 * s:256 * s + 256, :] = low
-            return D[...] + dot(SX[...], TH[...]) + dot(SX[...], TL[...])
-
-        def sweeps(value):
+                high, low = split(dot(jnp.concatenate([high, low], axis=1), SY[s]))
+                TT[256 * s:256 * s + 256, :] = high
+                TT[768 + 256 * s:1024 + 256 * s, :] = low
+            return D[...] + dot(SX[...], TT[...])
+
+        def stack_columns(value):
             high, low = split(value)
             for c in range(NCLASS):
                 keep = column_class == c
-                AH[256 * c:256 * c + 256, :] = jnp.where(keep, high, jnp.zeros_like(high))
-                AL[256 * c:256 * c + 256, :] = jnp.where(keep, low, jnp.zeros_like(low))
-            swept = dot(XH[...], AH[...]) + dot(XL[...], AH[...]) + dot(XH[...], AL[...])
+                AA[256 * c:256 * c + 256, :] = jnp.where(keep, high, jnp.zeros_like(high))
+                AA[1024 + 256 * c:1280 + 256 * c, :] = jnp.where(keep, low, jnp.zeros_like(low))
+
+        def sweeps(r, n):
+            rows = slice(r, r + n)
+            swept = dot(XHH[rows, :], AA[...]) + dot(XL[rows, :], AA[0:1024, :])
             high, low = split(swept)
             for c in range(NCLASS):
-                keep = row_class == c
-                BH[:, 256 * c:256 * c + 256] = jnp.where(keep, high, jnp.zeros_like(high))
-                BL[:, 256 * c:256 * c + 256] = jnp.where(keep, low, jnp.zeros_like(low))
-            return dot(BH[...], YH[...]) + dot(BL[...], YH[...]) + dot(BH[...], YL[...])
+                keep = row_class[rows] == c
+                BB[rows, 256 * c:256 * c + 256] = jnp.where(keep, high, jnp.zeros_like(high))
+                BB[rows, 1024 + 256 * c:1280 + 256 * c] = jnp.where(keep, low, jnp.zeros_like(low))
+            return dot(BB[rows, :], YHH[...]) + dot(BB[rows, 0:1024], YL[...])
 
         wait_for(A, ars)
-        D[...] = unpacked(A)
-        wait_for(L.at[0], lrs.at[0])
-        D[...] = sweeps(add_source(0))
-        wait_for(L.at[1], lrs.at[1])
-        result = sweeps(add_source(1))
-        for h in range(2):
-            rows = result[:, 128 * h:128 * h + 128].reshape(16, 2, 8, 128)
-            a, b = pair_swap(rows[:, 0].reshape(128, 128), rows[:, 1].reshape(128, 128))
-            R[:, 256 * h:256 * h + 128] = a
-            R[:, 256 * h + 128:256 * h + 256] = b
-
-        for dx, dy in far_first():
-            tx, ty = rem(x + dx, 4), rem(y + dy, 4)
-            for i in range(4):
-                zl = rem(z + 2 + i, 4)
-                rows = pl.ds(pl.multiple_of((4 * zl + ty) * 8, 8), 8)
-                src = R.at[rows, pl.ds(pl.multiple_of(tx * 128, 128), 128)]
-                copy = remote(src, Q.at[my_o], rss, rrs, (3, 4 * zl + ty, tx))
-                if dx or dy:
-                    copy.start()
-                    continue
-                mine = (sec == 3) & (zl == my_zl)
-
-                @pl.when(jnp.logical_not(mine))
-                def _():
-                    copy.start()
-
-                @pl.when(mine)
-                def _():
-                    pltpu.make_async_copy(src, Q.at[my_o], rrs).start()
+        D[...] = unpacked(A.reshape(128, 512))
+        stack_columns(add_source(0))
+        D[...] = sweeps(0, 256)
+        stack_columns(add_source(1))
+        for part in range(PARTS):
+            n = 256 // PARTS
+            result = sweeps(part * n, n)
+            for h in range(2):
+                rows = result[:, 128 * h:128 * h + 128].reshape(n // 16, 2, 8, 128)
+                a, b = pair_swap(rows[:, 0].reshape(n // 2, 128), rows[:, 1].reshape(n // 2, 128))
+                R[part * n // 2:(part + 1) * n // 2, 256 * h:256 * h + 128] = a
+                R[part * n // 2:(part + 1) * n // 2, 256 * h + 128:256 * h + 256] = b
+            for dx, dy in far_first():
+                tx, ty = rem(x + dx, 4), rem(y + dy, 4)
+                for zl in range(part * 4 // PARTS, (part + 1) * 4 // PARTS):
+                    rows = pl.ds(pl.multiple_of((4 * zl + ty) * 8, 8), 8)
+                    src = R.at[rows, pl.ds(pl.multiple_of(tx * 128, 128), 128)]
+                    copy = remote(src, Q.at[my_o], rss, rrs.at[div(my_m, 2)], (3, 4 * zl + ty, tx))
+                    if dx or dy:
+                        copy.start()
+                        continue
+                    mine = (sec == 3) & (zl == my_zl)
+
+                    @pl.when(jnp.logical_not(mine))
+                    def _():
+                        copy.start()
+
+                    @pl.when(mine)
+                    def _():
+                        pltpu.make_async_copy(src, Q.at[my_o], rrs.at[div(my_m, 2)]).start()
 
     @pl.when(sec == 3)
     def _():
-        wait_for(Q, rrs)
-
         def body(k, carry):
             blocks = []
+            wait_for(Q.at[pl.ds(0, 32)], rrs.at[k])
             for q in range(16):
                 a, b = pair_swap(Q[32 * k + q], Q[32 * k + 16 + q])
                 blocks.append(jnp.concatenate([a, b], axis=0))
@@ -518,6 +537,9 @@
             return carry
 
         lax.fori_loop(0, 3, body, 0)
+
+    @pl.when(sec == 3)
+    def _():
         drain_pieces(0)
 
     @pl.when(is_owner & (sec == 3))
@@ -548,22 +570,22 @@
     out = pl.pallas_call(
         kernel,
         out_shape=jax.ShapeDtypeStruct((3, 16, 2048), F32),
-        in_specs=[smem, smem, vmem, any_space, any_space, vmem, vmem],
+        in_specs=[smem, smem, any_space, any_space, any_space, vmem, vmem],
         out_specs=vmem,
         scratch_shapes=[
-            V((3, 24, 2560), F32), V((3, 32, 2560), F32), V((3, 16, 2048), F32),
+            V((3, 16, 2048), F32), V((3, 24, 2560), F32), V((3, 32, 2560), F32), V((3, 16, 2048), F32),
             V((2, 3, 8, 512), F32), V((2, 3, 8, 512), F32), V((2, 3, 16, 128), F32),
             V((8, 8, 128), F32), V((8, 8, 128), F32),
-            V((2, 96, 8, 128), F32), V((128, 512), F32), V((2, 3, 128, 512), F32),
+            V((2, 96, 8, 128), F32), V((4, 4, 8, 512), F32), V((2, 3, 128, 512), F32),
             V((4, 4, 4, 16, 256), F32), V((4, 256, 256), F32), V((4, 4, 16, 128), F32), V((8, 512), F32),
             V((16, 128), F32), V((8, 128), F32),
             V((128, 512), F32), V((256, 256), F32), V((96, 8, 128), F32),
-            V((256, 1024), BF16), V((256, 1024), BF16), V((1024, 256), BF16), V((1024, 256), BF16),
-            V((256, 768), BF16), V((3, 256, 256), BF16), V((768, 256), BF16), V((768, 256), BF16),
-            V((1024, 256), BF16), V((1024, 256), BF16), V((256, 1024), BF16), V((256, 1024), BF16),
-            D((8,)), D((8,)), D((2,)), D, D((2,)),
-            D((7,)), D((3,)), D((7,)), D((3,)), D, D, D, D, D, D, D, D,
-            pltpu.SemaphoreType.REGULAR, pltpu.SemaphoreType.REGULAR, pltpu.SemaphoreType.REGULAR,
+            V((256, 2048), BF16), V((256, 1024), BF16), V((2048, 256), BF16), V((1024, 256), BF16),
+            V((256, 1536), BF16), V((3, 512, 256), BF16), V((1536, 256), BF16),
+            V((2048, 256), BF16), V((256, 2048), BF16),
+            D, D((8,)), D((8,)), D((2,)), D, D((2, 3)),
+            D((7,)), D((3,)), D((7,)), D((3,)), D, D, D, D, D, D, D, D((3,)),
+            pltpu.SemaphoreType.REGULAR, pltpu.SemaphoreType.REGULAR,
         ],
         compiler_params=pltpu.CompilerParams(
             collective_id=0, has_side_effects=True, vmem_limit_bytes=60 << 20

time: 51.2 us -> 49.4 us (0.965)
  Pallas kernels: 49.1 us -> 47.4 us
    pallas_call x1, Pallas kernels: 49.1 us -> 47.4 us  [local(): pl.pallas_call(kernel, out_shape=jax.ShapeDtypeStruct((3, 16, 2048), F32)...]
where the time goes in v5:
time: 49.4 us; the launch traced here: 49.2 us
  Pallas kernels  47.4 us (96%)
  local copies, waits for them, and re-layouts  1.77 us (4%)
    pallas_call x1, Pallas kernels, local(): pl.pallas_call(kernel, out_shape=jax.ShapeDtypeStruct((3, 16, 2048), F32)...  47.4 us
    unnamed x1, local copies, waits for them, and re-layouts  1.77 us

profile of v5, /device:TPU:161, one launch (start us, length us, event | category | flops | bytes accessed | tf_op | source)
XLA Modules:
  0.0 49.2 jit_solution(10013541763460888801)
XLA Ops:
  0.0 47.4 %shard_map.73 = f32[3,16,2048]{2,1,0:T(8,128)} custom-call(f32[3,3,3]{2,1,0:T(4,128)} %coup.1, s32[2,3]{1,0:T(2,128)} %bitcast.7, f32[3,16,2048]{2,1,0:T(8,128)} %bitcast.6, f32[4,3,16,256]{3,2,1,0:T(8,128)} %xo.1, f32[4,3,64,256]{3,2,1,0:T(8,128)} %yo.1, s32[1,64]{1,0:T(1,128)} %bitcast.8, s32[1,16]{1,0:T(1,128)} %bitcast.9), custom_call_target="tpu_custom_call" | custom-call | tf_op jit(solution)/shard_map/pallas_call | solution.py:570
  47.4 1.8 %copy.9 = f32[1,3,16,2048]{3,2,1,0:T(8,128)} copy(f32[1,3,16,2048]{3,2,1,0:T(8,128)} %bitcast.5) | data formatting | bytes 786432
